TPU v7x, 256 devices: a whole 4x4x8 slice. The times are simulated.
256 devices in a mesh: seq: 64 (over x, y, z_lo, core), tensor: 4 (over z_hi).
Axes of the slice: x: 4, y: 4, z: 8 (z_hi: 4, z_lo: 2; z = z_hi * 2 + z_lo), core: 2. Of those that a mesh axis runs over, the one named last changes fastest.
Arguments:
- tokens_in: bfloat16 [2, 8192, 1536], P(None, 'seq', 'tensor'), may hold values from -6 to 6
- query_weight: bfloat16 [1536, 512], P(None, 'tensor'), may hold values from -0.22963966 to 0.22963966
- key_weight: bfloat16 [1536, 512], P(None, 'tensor'), may hold values from -0.22963966 to 0.22963966
- value_weight: bfloat16 [1536, 1536], P(None, 'tensor'), may hold values from -0.15625 to 0.15625
- out_weight: bfloat16 [1536, 1536], P('tensor'), may hold values from -1.25 to 1.25
- conv_weight: bfloat16 [3, 1536, 1536], P(None, None, 'tensor'), may hold values from -0.09375 to 0.09375
- cotangent: bfloat16 [2, 8192, 1536], P(None, 'seq', 'tensor'), may hold values from -6 to 6
Outputs:
- block_out: bfloat16 [2, 8192, 1536], P(None, 'seq', 'tensor')
- conv_grad: bfloat16 [3, 1536, 1536], P(None, None, 'tensor')
- residual_grad: bfloat16 [2, 8192, 1536], P(None, 'seq', 'tensor')
All inputs are finite; a program needn't handle non-finite values.
Results may differ from a plain program's by a relative error of at most 0.017.
The roundings to bfloat16 on the way count: a program that leaves them out, or rounds other values in their place, can miss the bound.
Values may be sent and summed in bfloat16 or wider, within the bound.
A program may use at most 128 MiB of HBM per device.

v0:
```python
import jax
import jax.numpy as jnp
from jax import lax
from jax.sharding import PartitionSpec as P

KEY = 64
VAL = 192
CONV_DILATION = 64


eps_norm = 1e-05
root_half = 0.7071067811865476
inv_root_two_pi = 0.3989422804014327


def extended(cells, sides, width):
    for axis, dim in sides:
        count = lax.axis_size(axis)
        ends = count - 1
        head = lax.slice_in_dim(cells, 0, width, axis=dim)
        tail = lax.slice_in_dim(cells, cells.shape[dim] - width, cells.shape[dim], axis=dim)
        cells = jnp.concatenate(
            [
                lax.ppermute(tail, axis, [(i, (i + 1) % count) for i in range(ends)]),
                cells,
                lax.ppermute(head, axis, [((i + 1) % count, i) for i in range(ends)]),
            ],
            axis=dim,
        )
    return cells


def normalize(values):
    average = jnp.mean(values, axis=-1, keepdims=True)
    centred = values - average
    inv_spread = lax.rsqrt(jnp.mean(centred * centred, axis=-1, keepdims=True) + eps_norm)
    return (centred * inv_spread, inv_spread)


def gelu_exact(values):
    return 0.5 * values * (1.0 + lax.erf(values * root_half))


def gelu_slope(values):
    return 0.5 * (1.0 + lax.erf(values * root_half)) + values * inv_root_two_pi * jnp.exp(
        -0.5 * values * values
    )


def body(tokens_in, query_weight, key_weight, value_weight, out_weight, conv_weight, cotangent):
    seq_count, position_offset, local_width = tokens_in.shape
    channel_width = local_width * lax.axis_size("tensor")
    local_heads = query_weight.shape[1] // KEY
    row_indices = seq_count * position_offset
    full_in = lax.all_gather(tokens_in, "tensor", axis=2, tiled=True)
    normed, _ = normalize(full_in.astype(jnp.float32))
    hidden = normed.astype(jnp.bfloat16).reshape(row_indices, channel_width)
    queries = jnp.dot(hidden, query_weight, preferred_element_type=jnp.float32).astype(jnp.bfloat16)
    keys = jnp.dot(hidden, key_weight, preferred_element_type=jnp.float32).astype(jnp.bfloat16)
    values_all = jnp.dot(hidden, value_weight, preferred_element_type=jnp.float32).astype(
        jnp.bfloat16
    )
    query_heads = queries.reshape(seq_count, position_offset, local_heads, KEY)
    keys = keys.reshape(seq_count, position_offset, local_heads * KEY)
    values_all = values_all.reshape(seq_count, position_offset, local_heads * VAL)
    score_scale = KEY ** (-0.5)
    start_top = jnp.full((seq_count, position_offset, local_heads), -jnp.inf, jnp.float32)
    start_total = jnp.zeros((seq_count, position_offset, local_heads), jnp.float32)
    start_acc = jnp.zeros((seq_count, position_offset, local_heads, VAL), jnp.float32)
    pieces = (
        lax.all_gather(keys, "seq", axis=1, tiled=True),
        lax.all_gather(values_all, "seq", axis=1, tiled=True),
    )
    count = pieces[0].shape[1]
    key_heads = pieces[0].reshape(seq_count, count, local_heads, KEY)
    value_heads = pieces[1].reshape(seq_count, count, local_heads, VAL)
    scores = (
        jnp.einsum("sqhd,skhd->sqhk", query_heads, key_heads, preferred_element_type=jnp.float32)
        * score_scale
    )
    new_top = jnp.max(scores, axis=-1)
    shrink = jnp.exp(start_top - new_top)
    weights = jnp.exp(scores - new_top[..., None])
    new_total = start_total * shrink + jnp.sum(weights, axis=-1)
    new_acc = start_acc * shrink[..., None] + jnp.einsum(
        "sqhk,skhv->sqhv",
        weights.astype(jnp.bfloat16),
        value_heads,
        preferred_element_type=jnp.float32,
    )
    attended = (
        (new_acc / new_total[..., None])
        .astype(jnp.bfloat16)
        .reshape(row_indices, local_heads * VAL)
    )
    partial_value = jnp.dot(attended, out_weight, preferred_element_type=jnp.float32).reshape(
        seq_count, position_offset, channel_width
    )
    mixed_local = lax.psum_scatter(
        partial_value.astype(jnp.bfloat16), "tensor", scatter_dimension=2, tiled=True
    ).astype(jnp.float32)
    block_in = (tokens_in.astype(jnp.float32) + mixed_local).astype(jnp.bfloat16)
    block_full = lax.all_gather(block_in, "tensor", axis=2, tiled=True)
    unit_normed, unit_inv = normalize(block_full.astype(jnp.float32))
    gelu_applied = gelu_exact(unit_normed).astype(jnp.bfloat16)
    units_padded = extended(gelu_applied, (("seq", 1),), CONV_DILATION)
    kernel_offsets = [
        units_padded[
            :, kernel_offset * CONV_DILATION : kernel_offset * CONV_DILATION + position_offset
        ].reshape(row_indices, channel_width)
        for kernel_offset in range(3)
    ]
    conv_out = jnp.zeros((row_indices, local_width), jnp.float32)
    for kernel_offset in range(3):
        conv_out = conv_out + jnp.dot(
            kernel_offsets[kernel_offset],
            conv_weight[kernel_offset],
            preferred_element_type=jnp.float32,
        )
    block_out = (
        block_in.astype(jnp.float32) + conv_out.reshape(seq_count, position_offset, local_width)
    ).astype(jnp.bfloat16)
    border_gradient = extended(cotangent, (("seq", 1),), CONV_DILATION)
    grad_rows = cotangent.reshape(row_indices, local_width)
    kernel_terms = jnp.stack(
        [
            jnp.einsum(
                "rc,rk->ck",
                kernel_offsets[kernel_offset],
                grad_rows,
                preferred_element_type=jnp.float32,
            )
            for kernel_offset in range(3)
        ]
    )
    position_scale = (row_indices * lax.axis_size("seq")) ** (-0.5)
    conv_grad = (lax.psum(kernel_terms, "seq") * position_scale).astype(jnp.bfloat16)
    unit_terms = jnp.zeros((row_indices, channel_width), jnp.float32)
    for kernel_offset in range(3):
        shifted_units = border_gradient[
            :,
            (2 - kernel_offset) * CONV_DILATION : (2 - kernel_offset) * CONV_DILATION
            + position_offset,
        ].reshape(row_indices, local_width)
        unit_terms = unit_terms + jnp.einsum(
            "rk,ck->rc",
            shifted_units,
            conv_weight[kernel_offset],
            preferred_element_type=jnp.float32,
        )
    unit_terms = unit_terms.reshape(seq_count, position_offset, channel_width)
    unit_grad = lax.psum(unit_terms.astype(jnp.bfloat16), "tensor").astype(jnp.float32)
    slope_grad = unit_grad * gelu_slope(unit_normed)
    first_mean = jnp.sum(slope_grad, axis=-1, keepdims=True) / channel_width
    second_mean = jnp.sum(slope_grad * unit_normed, axis=-1, keepdims=True) / channel_width
    full_grad = (slope_grad - first_mean - unit_normed * second_mean) * unit_inv
    input_grad = lax.dynamic_slice_in_dim(
        full_grad, lax.axis_index("tensor") * local_width, local_width, 2
    )
    residual_grad = (cotangent.astype(jnp.float32) + input_grad).astype(jnp.bfloat16)
    return (block_out, conv_grad, residual_grad)


def solution(mesh):
    placed = (
        P(None, "seq", "tensor"),
        P(None, "tensor"),
        P(None, "tensor"),
        P(None, "tensor"),
        P("tensor", None),
        P(None, None, "tensor"),
        P(None, "seq", "tensor"),
    )
    return jax.shard_map(
        body,
        mesh=mesh,
        in_specs=placed,
        out_specs=(P(None, "seq", "tensor"), P(None, None, "tensor"), P(None, "seq", "tensor")),
        check_vma=False,
    )
```

profile of v0, /device:TPU:1, one launch (start us, length us, event | category | flops | bytes accessed | tf_op | source)
XLA Modules:
  0.0 998.5 jit_solution(3490123864890254360)
XLA Ops:
  7.2 24.2 %all_gather.12 = bf16[2,128,1536]{2,1,0:T(8,128)(2,1)S(1)} all-gather(bf16[2,128,384]{2,1,0:T(8,128)(2,1)} %param.7), channel_id=1, replica_groups=mesh['seq'=64,'tensor'=4] {'tensor'}, dimensions={2}, use_global_device_ids=true | all-gather | bytes 983040 | tf_op jit(solution)/shard_map/all_gather | solution.py:55
  31.4 0.2 convert_reduce_fusion.1
  31.6 0.3 fusion.14
  32.0 0.3 fusion.15
  32.3 0.1 copy-done.8
  32.4 1.0 convolution_convert_fusion.3
  33.4 0.0 all-gather.5.cloned.1.call-start
  33.5 1.3 convolution_convert_fusion.1
  34.7 0.0 reduce-scatter.4.cloned.1.call-start
  34.8 0.4 convolution_convert_fusion.2
  35.2 0.1 reshape.112
  35.3 108.0 %all-gather.3.cloned.1.call-done = bf16[2,8192,128]{2,1,0:T(8,128)(2,1)} async-done(((bf16[2,128,128]{2,1,0:T(8,128)(2,1)}), bf16[2,8192,128]{2,1,0:T(8,128)(2,1)}) %all-gather.3.cloned.1.call-update) | async-done | bytes 4194320 | tf_op jit(solution)/shard_map/all_gather | solution.py:71
  143.2 6.3 copy.56
  149.6 11.1 %bitcast_reduce_fusion = (f32[2,128,2]{1,2,0:T(2,128)S(1)}, f32[2,2,8192,128]{3,2,1,0:T(8,128)}) fusion(bf16[2,8192,2,64]{1,3,2,0:T(8,128)(2,1)} %bitcast.95, bf16[2,128,2,64]{3,2,1,0:T(2,128)(2,1)S(1)} %reshape.112), kind=kOutput, calls=%fused_computation.1 | convolution fusion | flops 545259008 | bytes 21039104 | tf_op jit(solution)/shard_map/sqhd,skhd->sqhk/dot_general | solution.py:78
  160.7 8.7 fusion.1
  169.4 93.5 %all-gather.5.cloned.1.call-done = bf16[2,8192,384]{2,1,0:T(8,128)(2,1)} async-done(((bf16[2,128,384]{2,1,0:T(8,128)(2,1)}), bf16[2,8192,384]{2,1,0:T(8,128)(2,1)}) %all-gather.5.cloned.1.call-update) | async-done | bytes 12582928 | tf_op jit(solution)/shard_map/all_gather | solution.py:72
  263.0 15.6 %copy.59 = bf16[2,8192,384]{1,2,0:T(8,128)(2,1)} copy(bf16[2,8192,384]{2,1,0:T(8,128)(2,1)} %all-gather.5.cloned.1.call-done) | data formatting | bytes 25165824 | tf_op jit(solution)/shard_map/all_gather | solution.py:72
  278.6 13.2 %fusion.39 = bf16[2,128,2,192]{1,3,2,0:T(8,128)(2,1)S(1)} fusion(bf16[2,8192,2,192]{1,3,2,0:T(8,128)(2,1)} %bitcast.94, f32[2,2,8192,128]{3,2,1,0:T(8,128)} %get-tuple-element.28, f32[2,128,2]{1,2,0:T(2,128)S(1)} %get-tuple-element.27, f32[2,128,2]{1,2,0:T(2,128)S(1)} %get-tuple-element.26, f32[2,128,2]{1,2,0:T(2,128)S(1)} %get-tuple-element.25), kind=kOutput, calls=%fused_computation.54 | convolution fusion | flops 1623490560 | bytes 29562880 | tf_op jit(solution)/shard_map/sqhk,skhv->sqhv/dot_general | solution.py:85
  291.9 0.6 convolution_convert_fusion
  292.5 0.6 copy.79
  293.1 1.0 copy.89
  294.2 2.3 collective-permute-start.2
  296.5 3.6 collective-permute-start.3
  300.1 1.9 fusion.29
  302.0 0.2 copy.55
  302.2 1.9 fusion.26
  304.1 1.9 fusion.8
  306.0 1.2 copy.72
  307.2 0.0 all-reduce.3.cloned.1.call-start
  307.3 14.7 %reduce-scatter.4.cloned.1.call-done = bf16[384,256]{1,0:T(8,128)(2,1)} async-done(((bf16[1536,256]{1,0:T(8,128)(2,1)}), bf16[384,256]{1,0:T(8,128)(2,1)}) %reduce-scatter.4.cloned.1.call-update) | async-done | bytes 196624
  322.0 1.0 reshape.114
  323.0 20.0 %all_gather.15 = bf16[2,128,1536]{1,2,0:T(8,128)(2,1)S(1)} all-gather(bf16[2,128,384]{1,2,0:T(8,128)(2,1)S(1)} %add_convert_fusion.1), channel_id=1, replica_groups=mesh['seq'=64,'tensor'=4] {'tensor'}, dimensions={2}, use_global_device_ids=true | all-gather | bytes 983040 | tf_op jit(solution)/shard_map/all_gather | solution.py:103
  343.0 0.2 convert_reduce_fusion
  343.2 0.2 fusion.13
  343.5 43.0 %all-reduce.5.cloned.1.call-done = bf16[2,128,1536]{1,2,0:T(8,128)(2,1)} async-done(((bf16[2,128,1536]{1,2,0:T(8,128)(2,1)}), bf16[2,128,1536]{1,2,0:T(8,128)(2,1)}) %all-reduce.5.cloned.1.call-update) | async-done | bytes 786448 | tf_op jit(solution)/shard_map/psum | solution.py:152
  386.5 3.9 fusion.56
  390.4 0.3 fusion.58
  390.6 1.0 copy.67
  391.7 3.3 collective-permute-start.1
  394.9 1.0 copy.63
  396.0 2.4 collective-permute-start
  398.3 0.6 convolution_bitcast_fusion.1
  398.9 2.2 collective-permute-done.1
  401.2 2.2 copy.68
  403.4 2.2 copy.64
  405.5 2.2 pad_maximum_fusion.1
  407.8 0.6 convolution_bitcast_fusion
  408.4 0.3 copy-done.3
  408.7 0.2 copy-done.5
  408.9 0.6 convolution_bitcast_fusion.2
  409.5 3.6 pad_maximum_fusion
  413.0 0.2 copy.71
  413.2 0.3 copy.66
  413.5 1.3 fusion.51
  414.8 0.8 copy.74
  415.7 1.2 copy.65
  416.8 0.3 copy.69
  417.1 2.1 fusion.33
  419.2 1.8 convolution_add_fusion.2
  421.1 1.8 convolution_add_fusion.1
  422.9 0.2 copy.70
  423.1 0.8 copy.73
  423.9 562.5 %all-reduce.3.cloned.1.call-done = f32[3,1536,384]{2,1,0:T(8,128)} async-done(((f32[3,1536,384]{2,1,0:T(8,128)}), f32[3,1536,384]{2,1,0:T(8,128)}) %all-reduce.3.cloned.1.call-update) | async-done | bytes 7077904 | tf_op jit(solution)/shard_map/psum | solution.py:137
  986.4 5.5 multiply_convert_fusion
  (39 shorter events, 0.4 us)
Async XLA Ops:
  7.2 284.7 %copy-start = (bf16[384,1536]{1,0:T(8,128)(2,1)S(1)}, bf16[384,1536]{1,0:T(8,128)(2,1)}, u32[]{:S(2)}) copy-start(bf16[384,1536]{1,0:T(8,128)(2,1)} %param.11) | copy-start | bytes 3538948
  7.2 136.1 %all-gather.3.cloned.1.call-start = ((), (), s32[]{:S(2)}) async-start(), calls=%async_computation.1 | async-start | bytes 4259840 | tf_op jit(solution)/shard_map/all_gather | solution.py:71
  31.4 1.0 copy-start.8
  31.9 1.5 copy-start.10
  32.4 2.4 copy-start.9
  33.4 229.6 %all-gather.5.cloned.1.call-start = ((), (), s32[]{:S(2)}) async-start(), calls=%async_computation.2 | async-start | bytes 12779520 | tf_op jit(solution)/shard_map/all_gather | solution.py:72
  34.7 287.2 %reduce-scatter.4.cloned.1.call-start = ((), (), s32[]{:S(2)}) async-start(), calls=%async_computation.5 | async-start | bytes 983040
  293.1 1.1 copy-start.2
  294.1 92.4 %all-reduce.5.cloned.1.call-start = ((), (), s32[]{:S(2)}) async-start(), calls=%async_computation.4 | async-start | bytes 1572864 | tf_op jit(solution)/shard_map/psum | solution.py:152
  294.2 7.8 copy-start.7
  294.2 8.0 collective-permute-start.2
  296.5 5.6 collective-permute-start.3
  307.2 679.2 %all-reduce.3.cloned.1.call-start = ((), (), s32[]{:S(2)}) async-start(), calls=%async_computation.3 | async-start | bytes 14155776 | tf_op jit(solution)/shard_map/psum | solution.py:137
  391.7 9.5 collective-permute-start.1
  396.0 7.4 collective-permute-start
  407.8 0.9 copy-start.3
  407.8 1.1 copy-start.5
  413.2 2.4 copy-start.6
  413.5 3.3 copy-start.4
  986.4 5.5 copy-start.1
Sparse Core Ops, SparseCore 0:
  33.5 109.6 all-gather.2
  145.6 117.3 all-gather.4
  294.2 27.7 reduce-scatter.3
  324.5 61.9 all-reduce.4
  413.2 573.2 all-reduce.2
where the time goes:
time: 1000 us; the launch traced here: 998 us
  waiting for transfers between devices  824 us (82%)
  blocking collectives  44.2 us (4%)
  matrix products  40.7 us (4%)
  local copies, waits for them, and re-layouts  37 us (4%)
  other arithmetic  26.6 us (3%)
  between operations  14.1 us (1%)
  starting transfers between devices  11.7 us (1%)
    psum x1, waiting for transfers between devices, body(): lax.psum(kernel_terms, 'seq') * position_scale  562 us
    all_gather x1, waiting for transfers between devices, body(): lax.all_gather(keys, 'seq', axis=1, tiled=True)  108 us
    all_gather x1, waiting for transfers between devices, body(): lax.all_gather(values_all, 'seq', axis=1, tiled=True)  93.5 us
    psum x1, waiting for transfers between devices, body(): lax.psum(unit_terms.astype(jnp.bfloat16), 'tensor').astype(jnp.float32)  43 us
    all_gather x1, blocking collectives, body(): full_in = lax.all_gather(tokens_in, 'tensor', axis=2, tiled=True)  24.2 us
  transfers between devices with their start and end apart: 9, of which 6 were waited for; matrix products, arithmetic and copies ran while one was open for 5% of the time, Pallas kernels for 0%

commit v1 on v0

v1 whole, which is shorter than its diff:
```python
import functools

import jax
import jax.numpy as jnp
from jax import lax
from jax.experimental import pallas as pl
from jax.experimental.pallas import tpu as pltpu
from jax.sharding import PartitionSpec as P

KEY = 64
VAL = 192
CONV_DILATION = 64
NT = 4
NX, NY, NZ, NC = 4, 4, 2, 2

eps_norm = 1e-05
root_half = 0.7071067811865476
inv_root_two_pi = 0.3989422804014327

MESH = pl.DeviceIdType.MESH
BF = jnp.bfloat16
F32 = jnp.float32
VMEM = pltpu.VMEM
VSPEC = pl.BlockSpec(memory_space=pltpu.VMEM)
VMEM_LIMIT = 60 * 1024 * 1024


def normalize(values):
    average = jnp.mean(values, axis=-1, keepdims=True)
    centred = values - average
    inv_spread = lax.rsqrt(jnp.mean(centred * centred, axis=-1, keepdims=True) + eps_norm)
    return (centred * inv_spread, inv_spread)


def gelu_exact(values):
    return 0.5 * values * (1.0 + lax.erf(values * root_half))


def gelu_slope(values):
    return 0.5 * (1.0 + lax.erf(values * root_half)) + values * inv_root_two_pi * jnp.exp(
        -0.5 * values * values
    )


def seq_pos():
    s = lax.axis_index("seq")
    core = lax.rem(s, 2)
    z = lax.rem(lax.div(s, 2), 2)
    y = lax.rem(lax.div(s, 4), 4)
    x = lax.div(s, 16)
    return x, y, z, core


def seq_dev(x, y, z, core):
    return ((x * NY + y) * NZ + z) * NC + core


def nxt(i, k):
    return lax.rem(i + k, 4)


class Sender:
    def __init__(self, send_sems, recv_sems):
        self.ss, self.rs, self.n, self.flying = send_sems, recv_sems, 0, []

    def make(self, src, dst, dev):
        i = self.n
        self.n += 1
        return pltpu.make_async_remote_copy(
            src_ref=src,
            dst_ref=dst,
            send_sem=self.ss.at[i],
            recv_sem=self.rs.at[i],
            device_id=dev,
            device_id_type=MESH,
        )

    def go(self, src, dst, dev):
        c = self.make(src, dst, dev)
        c.start()
        self.flying.append(c)
        return c

    def drain(self):
        for c in self.flying:
            c.wait_send()
        self.flying = []


def greet(devs):
    barrier = pltpu.get_barrier_semaphore()
    for d in devs:
        pl.semaphore_signal(barrier, inc=1, device_id=d, device_id_type=MESH)
    pl.semaphore_wait(barrier, len(devs))


class Gather4:
    def __init__(self, sender, view, me, plus, minus, on_block=None):
        self.s, self.view, self.me, self.plus, self.minus = sender, view, me, plus, minus

    def begin(self):
        s, v, me = self.s, self.view, self.me
        self.c0 = s.go(v(me, 0), v(me, 0), self.plus)
        self.c2 = s.go(v(me, 1), v(me, 1), self.minus)
        self.c1 = s.go(v(me, 1), v(me, 1), self.plus)
        self.c3 = s.go(v(me, 0), v(me, 0), self.minus)

    def relay(self):
        s, v, me = self.s, self.view, self.me
        self.c0.wait_recv()
        self.c4 = s.go(v(nxt(me, 3), 0), v(nxt(me, 3), 0), self.plus)
        self.c2.wait_recv()
        self.c5 = s.go(v(nxt(me, 1), 1), v(nxt(me, 1), 1), self.minus)

    def wait_near(self):
        self.c1.wait_recv()
        self.c3.wait_recv()

    def wait_far(self):
        self.c4.wait_recv()
        self.c5.wait_recv()


class Reduce4:
    def __init__(self, sender, x, rbuf, me, plus, minus):
        self.s, self.x, self.r, self.me, self.plus, self.minus = sender, x, rbuf, me, plus, minus

    def begin(self):
        s, x, r, me = self.s, self.x, self.r, self.me
        self.a0 = s.go(x(nxt(me, 2), 0), r(0, 0), self.plus)
        self.a1 = s.go(x(nxt(me, 2), 1), r(1, 1), self.minus)
        self.b0 = s.go(x(nxt(me, 1), 1), r(2, 1), self.plus)
        self.b1 = s.go(x(nxt(me, 3), 0), r(3, 0), self.minus)

    def combine(self):
        s, x, r, me = self.s, self.x, self.r, self.me
        self.a0.wait_recv()
        t0 = r(6, 0)
        t0[...] = (x(nxt(me, 1), 0)[...].astype(F32) + r(0, 0)[...].astype(F32)).astype(BF)
        self.c0 = s.go(t0, r(4, 0), self.plus)
        self.a1.wait_recv()
        t1 = r(7, 1)
        t1[...] = (x(nxt(me, 3), 1)[...].astype(F32) + r(1, 1)[...].astype(F32)).astype(BF)
        self.c1 = s.go(t1, r(5, 1), self.minus)

    def finish(self):
        x, r, me = self.x, self.r, self.me
        self.b0.wait_recv()
        self.b1.wait_recv()
        self.c0.wait_recv()
        h0 = x(me, 0)[...].astype(F32) + r(3, 0)[...].astype(F32) + r(4, 0)[...].astype(F32)
        self.c1.wait_recv()
        h1 = x(me, 1)[...].astype(F32) + r(2, 1)[...].astype(F32) + r(5, 1)[...].astype(F32)
        return h0, h1


def tensor_ring():
    t = lax.axis_index("tensor")
    return t, {"tensor": nxt(t, 1)}, {"tensor": nxt(t, 3)}


def params(cid):
    return pltpu.CompilerParams(
        collective_id=cid, has_side_effects=True, vmem_limit_bytes=VMEM_LIMIT
    )


def project_kernel(tok_ref, wq_ref, wk_ref, wv_ref, q_ref, kv_ref, full, ss, rs):
    t, plus, minus = tensor_ring()
    rows, width = tok_ref.shape
    half = rows // 2
    greet([plus, minus])

    def view(slot, h):
        return full.at[slot, pl.ds(h * half, half)]

    full[t] = tok_ref[...]
    s = Sender(ss, rs)
    g = Gather4(s, view, t, plus, minus)
    g.begin()
    g.relay()
    g.wait_near()
    g.wait_far()
    values = jnp.concatenate([full[i] for i in range(NT)], axis=1).astype(F32)
    hidden = normalize(values)[0].astype(BF)
    q_ref[...] = jnp.dot(hidden, wq_ref[...], preferred_element_type=F32).astype(BF)
    keys = q_ref.shape[1]
    kv_ref[:, :keys] = jnp.dot(hidden, wk_ref[...], preferred_element_type=F32).astype(BF)
    kv_ref[:, keys:] = jnp.dot(hidden, wv_ref[...], preferred_element_type=F32).astype(BF)
    s.drain()


def project(tokens, wq, wk, wv):
    rows, width = tokens.shape
    return pl.pallas_call(
        project_kernel,
        name="project",
        out_shape=(
            jax.ShapeDtypeStruct((rows, wq.shape[1]), BF),
            jax.ShapeDtypeStruct((rows, wk.shape[1] + wv.shape[1]), BF),
        ),
        in_specs=[VSPEC] * 4,
        out_specs=(VSPEC, VSPEC),
        scratch_shapes=[
            VMEM((NT, rows, width), BF),
            pltpu.SemaphoreType.DMA((6,)),
            pltpu.SemaphoreType.DMA((6,)),
        ],
        compiler_params=params(1),
    )(tokens, wq, wk, wv)


def attention_kernel(q_ref, kv_ref, out_ref, qbuf, kvbuf, obuf, orecv, lbuf, lrecv, ss, rs):
    x, y, z, core = seq_pos()
    count = q_ref.shape[1]
    partner = {"seq": seq_dev(x, y, z, 1 - core)}
    zpeer = {"seq": seq_dev(x, y, 1 - z, core)}
    xs = [{"seq": seq_dev(nxt(x, k), y, z, core)} for k in (1, 2, 3)]
    ys = [{"seq": seq_dev(x, nxt(y, k), z, core)} for k in (1, 2, 3)]
    greet([partner, zpeer] + xs + ys)
    s = Sender(ss, rs)
    half = count // 2
    axes = ((x, xs, y, ys), (y, ys, x, xs))
    state = []
    for i, (a, a_dev, b, b_dev) in enumerate(axes):
        kvbuf[i, a, z, core] = kv_ref[i]
        qbuf[i, b] = q_ref[i]

    for i, (a, a_dev, b, b_dev) in enumerate(axes):
        own = kvbuf.at[i, a, z, core]
        cz = s.go(own, own, zpeer)

        def kview(slot, h, i=i, zz=z):
            return kvbuf.at[i, slot, zz, core, pl.ds(h * half, half)]

        def oview(slot, h, i=i, zz=1 - z):
            return kvbuf.at[i, slot, zz, core, pl.ds(h * half, half)]

        def qview(slot, h, i=i):
            return qbuf.at[i, slot, pl.ds(h * half, half)]

        gk = Gather4(s, kview, a, a_dev[0], a_dev[2])
        go = Gather4(s, oview, a, a_dev[0], a_dev[2])
        gq = Gather4(s, qview, b, b_dev[0], b_dev[2])
        gq.begin()
        gk.begin()
        fw = [s.go(own, own, partner)]
        state.append((cz, gk, go, gq, fw))
    for i, (a, a_dev, b, b_dev) in enumerate(axes):
        cz, gk, go, gq, fw = state[i]
        cz.wait_recv()
        go.begin()
        mine = kvbuf.at[i, a, 1 - z, core]
        fw.append(s.go(mine, mine, partner))
        gq.relay()
        gk.relay()
    for i, (a, a_dev, b, b_dev) in enumerate(axes):
        cz, gk, go, gq, fw = state[i]
        gk.wait_near()
        for k in (1, 3):
            ref = kvbuf.at[i, nxt(a, k), z, core]
            fw.append(s.go(ref, ref, partner))
        go.relay()
        gk.wait_far()
        ref = kvbuf.at[i, nxt(a, 2), z, core]
        fw.append(s.go(ref, ref, partner))
    for i, (a, a_dev, b, b_dev) in enumerate(axes):
        cz, gk, go, gq, fw = state[i]
        go.wait_near()
        for k in (1, 3):
            ref = kvbuf.at[i, nxt(a, k), 1 - z, core]
            fw.append(s.go(ref, ref, partner))
        go.wait_far()
        ref = kvbuf.at[i, nxt(a, 2), 1 - z, core]
        fw.append(s.go(ref, ref, partner))
        gq.wait_near()
        gq.wait_far()
    lane = lax.broadcasted_iota(jnp.int32, (count, 128), 1)
    scale = KEY ** (-0.5)
    keys = NX * NZ * NC * count
    sent = []
    for i, (a, a_dev, b, b_dev) in enumerate(axes):
        for f in state[i][4]:
            f.wait_recv()

        @pl.loop(0, 4)
        def _(r, i=i):
            q = qbuf[i, r]
            k = kvbuf[i, :, :, :, :, 0:128].reshape(keys, 128)
            parts = []
            stats = jnp.zeros((count, 128), F32)
            for h in range(2):
                qh = jnp.where((lane < KEY) if h == 0 else (lane >= KEY), q, jnp.zeros_like(q))
                sc = (
                    lax.dot_general(
                        qh, k, (((1,), (1,)), ((), ())), preferred_element_type=F32
                    )
                    * scale
                )
                top = jnp.max(sc, axis=-1, keepdims=True)
                w = jnp.exp(sc - top)
                total = jnp.sum(w, axis=-1, keepdims=True)
                v = kvbuf[i, :, :, :, :, 128 + 128 * h : 384 + 128 * h].reshape(keys, 256)
                acc = jnp.dot(w.astype(BF), v, preferred_element_type=F32) / total
                parts.append(acc)
                stats = jnp.where(lane == h, top + jnp.log(total), stats)
            obuf[i, r, :, 0:128] = parts[0][:, :128].astype(BF)
            obuf[i, r, :, 128:256] = jnp.where(
                lane < 64, parts[0][:, 128:], parts[1][:, :128]
            ).astype(BF)
            obuf[i, r, :, 256:384] = parts[1][:, 128:].astype(BF)
            lbuf[i, r] = stats.T[0:8]

        for k in (2, 1, 3):
            dev = b_dev[k - 1]
            sent.append(s.go(obuf.at[i, nxt(b, k)], orecv.at[i, b], dev))
            sent.append(s.go(lbuf.at[i, nxt(b, k)], lrecv.at[i, b], dev))
        orecv[i, b] = obuf[i, b]
        lrecv[i, b] = lbuf[i, b]
    for c in sent:
        c.wait_recv()
    for i in range(2):
        logs = []
        for r in range(4):
            wide = jnp.concatenate([lrecv[i, r], jnp.zeros((120, 128), F32)], axis=0).T
            logs.append([wide[:, h : h + 1] for h in range(2)])
        wts = []
        for h in range(2):
            top = logs[0][h]
            for r in range(1, 4):
                top = jnp.maximum(top, logs[r][h])
            e = [jnp.exp(logs[r][h] - top) for r in range(4)]
            total = e[0] + e[1] + e[2] + e[3]
            wts.append([er / total for er in e])
        for g in range(3):
            acc = jnp.zeros((count, 128), F32)
            for r in range(4):
                if g == 0:
                    w = wts[0][r]
                elif g == 2:
                    w = wts[1][r]
                else:
                    w = jnp.where(lane < 64, wts[0][r], wts[1][r])
                acc = acc + orecv[i, r, :, 128 * g : 128 * g + 128].astype(F32) * w
            out_ref[i, :, 128 * g : 128 * g + 128] = acc.astype(BF)
    s.drain()


def attention(q, kv):
    seqs, count, keys = q.shape
    vals = kv.shape[2] - keys
    n = 2 * (1 + 6 * 3 + 8 + 6)
    return pl.pallas_call(
        attention_kernel,
        name="attention",
        out_shape=jax.ShapeDtypeStruct((seqs, count, vals), BF),
        in_specs=[VSPEC] * 2,
        out_specs=VSPEC,
        scratch_shapes=[
            VMEM((seqs, 4, count, keys), BF),
            VMEM((seqs, 4, NZ, NC, count, keys + vals), BF),
            VMEM((seqs, 4, count, vals), BF),
            VMEM((seqs, 4, count, vals), BF),
            VMEM((seqs, 4, 8, count), F32),
            VMEM((seqs, 4, 8, count), F32),
            pltpu.SemaphoreType.DMA((n,)),
            pltpu.SemaphoreType.DMA((n,)),
        ],
        compiler_params=params(2),
    )(q, kv)


def tensor_sum_kernel(terms_ref, *refs, has_base):
    if has_base:
        base_ref, out_ref, rbuf, ss, rs = refs
    else:
        out_ref, rbuf, ss, rs = refs
    t, plus, minus = tensor_ring()
    rows = terms_ref.shape[1]
    half = rows // 2
    greet([plus, minus])
    s = Sender(ss, rs)

    def x(p, h):
        return terms_ref.at[p, pl.ds(h * half, half)]

    red = Reduce4(s, x, lambda i, h: rbuf.at[i], t, plus, minus)
    red.begin()
    red.combine()
    parts = red.finish()
    for h in range(2):
        part = parts[h]
        if has_base:
            part = part + base_ref[h * half : (h + 1) * half].astype(F32)
        out_ref[t, pl.ds(h * half, half)] = part.astype(BF)
    g = Gather4(s, lambda p, h: out_ref.at[p, pl.ds(h * half, half)], t, plus, minus)
    g.begin()
    g.relay()
    g.wait_near()
    g.wait_far()
    s.drain()


def tensor_sum(terms, base, cid):
    _, rows, width = terms.shape
    args = (terms,) if base is None else (terms, base)
    return pl.pallas_call(
        functools.partial(tensor_sum_kernel, has_base=base is not None),
        name="tensor_sum_%d" % cid,
        out_shape=jax.ShapeDtypeStruct(terms.shape, BF),
        in_specs=[VSPEC] * len(args),
        out_specs=VSPEC,
        scratch_shapes=[
            VMEM((8, rows // 2, width), BF),
            pltpu.SemaphoreType.DMA((12,)),
            pltpu.SemaphoreType.DMA((12,)),
        ],
        compiler_params=params(cid),
    )(*args)


def conv_grad_kernel(
    units_ref, cot_ref, out_ref, send, recv, sums, r1, mid, r2, fin, zrecv, ss, rs
):
    x, y, z, core = seq_pos()
    width = units_ref.shape[1]
    total = 3 * width
    mine = total // 2
    tile = 256
    tiles = mine // tile
    per_tap = width // tile

    def pick(u, v):
        return jnp.where(core == 0, u, v)

    a, b = pick(x, y), pick(y, x)

    def along_a(k):
        return {"seq": pick(seq_dev(nxt(x, k), y, z, core), seq_dev(x, nxt(y, k), z, core))}

    def along_b(k):
        return {"seq": pick(seq_dev(x, nxt(y, k), z, core), seq_dev(nxt(x, k), y, z, core))}

    partner = {"seq": seq_dev(x, y, z, 1 - core)}
    zpeer = {"seq": seq_dev(x, y, 1 - z, core)}
    ap, am, bp, bm = along_a(1), along_a(3), along_b(1), along_b(3)
    greet([partner, zpeer, ap, am, bp, bm])

    def product(g):
        tap = lax.div(g, per_tap)
        col = pl.multiple_of(lax.rem(g, per_tap) * tile, tile)
        return lax.dot_general(
            units_ref[:, pl.ds(col, tile)],
            cot_ref[tap],
            (((0,), (0,)), ((), ())),
            preferred_element_type=F32,
        )

    def exchange(i):
        return pltpu.make_async_remote_copy(
            src_ref=send.at[i],
            dst_ref=recv.at[i],
            send_sem=ss.at[i],
            recv_sem=rs.at[i],
            device_id=partner,
            device_id_type=MESH,
        )

    @pl.loop(0, tiles)
    def _(i):
        send[i] = product((1 - core) * tiles + i).astype(BF)
        exchange(i).start()

    @pl.loop(0, tiles)
    def _(i):
        own = product(core * tiles + i)
        exchange(i).wait_recv()
        row = pl.multiple_of(i * tile, tile)
        sums[pl.ds(row, tile)] = (own + recv[i].astype(F32)).astype(BF)

    s = Sender(ss, rs)
    s.n = tiles
    big = mine // 4
    small = big // 4
    bh = (0, big // 2)
    bn = (big // 2, big // 2)
    cut = (small // 2 + 15) // 16 * 16
    sh = (0, cut)
    sn = (cut, small - cut)

    def m16(v):
        return pl.multiple_of(v, 16)

    first = Reduce4(
        s,
        lambda p, h: sums.at[pl.ds(m16(p * big + bh[h]), bn[h])],
        lambda i, h: r1.at[i],
        a,
        ap,
        am,
    )
    first.begin()
    first.combine()
    h0, h1 = first.finish()
    mid[0 : big // 2] = h0.astype(BF)
    mid[big // 2 : big] = h1.astype(BF)
    second = Reduce4(
        s,
        lambda p, h: mid.at[pl.ds(m16(p * small + sh[h]), sn[h])],
        lambda i, h: r2.at[i, pl.ds(0, sn[h])],
        b,
        bp,
        bm,
    )
    second.begin()
    second.combine()
    h0, h1 = second.finish()
    fin[0:cut] = h0.astype(BF)
    fin[cut:small] = h1.astype(BF)
    cz = s.go(fin, zrecv, zpeer)
    cz.wait_recv()
    at = core * mine + a * big + b * small
    out_ref[pl.ds(m16(at), small)] = (fin[...].astype(F32) + zrecv[...].astype(F32)).astype(BF)
    g2 = Gather4(
        s,
        lambda p, h: out_ref.at[pl.ds(m16(core * mine + a * big + p * small + sh[h]), sn[h])],
        b,
        bp,
        bm,
    )
    g2.begin()
    g2.relay()
    g2.wait_near()
    g2.wait_far()

    def block(p):
        return out_ref.at[pl.ds(m16(core * mine + p * big), big)]

    g1 = Gather4(
        s,
        lambda p, h: out_ref.at[pl.ds(m16(core * mine + p * big + bh[h]), bn[h])],
        a,
        ap,
        am,
    )
    g1.begin()
    fw = [s.go(block(a), block(a), partner)]
    g1.relay()
    g1.wait_near()
    for k in (1, 3):
        fw.append(s.go(block(nxt(a, k)), block(nxt(a, k)), partner))
    g1.wait_far()
    fw.append(s.go(block(nxt(a, 2)), block(nxt(a, 2)), partner))
    for f in fw:
        f.wait_recv()
    s.drain()

    @pl.loop(0, tiles)
    def _(i):
        exchange(i).wait_send()


def conv_grad_sum(units, cots):
    rows, width = units.shape
    local = cots.shape[2]
    mine = 3 * width // 2
    big, small = mine // 4, mine // 16
    cut = (small // 2 + 15) // 16 * 16
    n = mine // 256 + 6 * 4 + 1 + 4
    return pl.pallas_call(
        conv_grad_kernel,
        name="conv_grad",
        out_shape=jax.ShapeDtypeStruct((3 * width, local), BF),
        in_specs=[VSPEC] * 2,
        out_specs=VSPEC,
        scratch_shapes=[
            VMEM((mine // 256, 256, local), BF),
            VMEM((mine // 256, 256, local), BF),
            VMEM((mine, local), BF),
            VMEM((8, big // 2, local), BF),
            VMEM((big, local), BF),
            VMEM((8, cut, local), BF),
            VMEM((small, local), BF),
            VMEM((small, local), BF),
            pltpu.SemaphoreType.DMA((n,)),
            pltpu.SemaphoreType.DMA((n,)),
        ],
        compiler_params=params(5),
    )(units, cots)


def from_neighbours(head, tail, axis):
    count = lax.axis_size(axis)
    ends = count - 1
    before = lax.ppermute(tail, axis, [(i, i + 1) for i in range(ends)])
    after = lax.ppermute(head, axis, [(i + 1, i) for i in range(ends)])
    return before, after


def body(tokens_in, query_weight, key_weight, value_weight, out_weight, conv_weight, cotangent):
    seqs, count, local = tokens_in.shape
    width = local * NT
    rows = seqs * count
    edge = CONV_DILATION
    q, kv = project(tokens_in.reshape(rows, local), query_weight, key_weight, value_weight)
    attended = attention(q.reshape(seqs, count, -1), kv.reshape(seqs, count, -1))

    before, after = from_neighbours(cotangent[:, :edge], cotangent[:, count - edge :], "seq")
    cot_ext = jnp.concatenate([before, cotangent, after], axis=1)
    cots = jnp.stack(
        [
            cot_ext[:, (2 - j) * edge : (2 - j) * edge + count].reshape(rows, local)
            for j in range(3)
        ]
    )
    unit_terms = jnp.einsum("jrk,jck->rc", cots, conv_weight, preferred_element_type=F32)
    unit_terms = unit_terms.astype(BF).reshape(rows, NT, local).transpose(1, 0, 2)
    unit_grad = tensor_sum(unit_terms, None, 3)

    mixed = jnp.dot(attended.reshape(rows, local), out_weight, preferred_element_type=F32)
    mixed = mixed.astype(BF).reshape(rows, NT, local).transpose(1, 0, 2)
    block_full = tensor_sum(mixed, tokens_in.reshape(rows, local), 4)
    t = lax.axis_index("tensor")
    block_in = lax.dynamic_index_in_dim(block_full, t, 0, keepdims=False)
    block_full = block_full.transpose(1, 0, 2).reshape(rows, width)
    unit_normed, unit_inv = normalize(block_full.astype(F32))
    units = gelu_exact(unit_normed).astype(BF)

    conv_grad = conv_grad_sum(units, cots)
    conv_grad = (conv_grad.astype(F32) * ((rows * lax.axis_size("seq")) ** (-0.5))).astype(BF)
    conv_grad = conv_grad.reshape(3, width, local)

    taps = [
        jnp.dot(units, conv_weight[j], preferred_element_type=F32).reshape(seqs, count, local)
        for j in range(3)
    ]
    before, after = from_neighbours(taps[2][:, :edge], taps[0][:, count - edge :], "seq")
    from_left = jnp.concatenate([before, taps[0][:, : count - edge]], axis=1)
    from_right = jnp.concatenate([taps[2][:, edge:], after], axis=1)
    conv_out = from_left + taps[1] + from_right
    block_out = (block_in.reshape(seqs, count, local).astype(F32) + conv_out).astype(BF)

    unit_grad = unit_grad.transpose(1, 0, 2).reshape(rows, width).astype(F32)
    slope_grad = unit_grad * gelu_slope(unit_normed)
    first_mean = jnp.sum(slope_grad, axis=-1, keepdims=True) / width
    second_mean = jnp.sum(slope_grad * unit_normed, axis=-1, keepdims=True) / width
    full_grad = (slope_grad - first_mean - unit_normed * second_mean) * unit_inv
    input_grad = lax.dynamic_slice_in_dim(full_grad, t * local, local, 1)
    residual_grad = (cotangent.astype(F32) + input_grad.reshape(seqs, count, local)).astype(BF)
    return (block_out, conv_grad, residual_grad)


def solution(mesh):
    placed = (
        P(None, "seq", "tensor"),
        P(None, "tensor"),
        P(None, "tensor"),
        P(None, "tensor"),
        P("tensor", None),
        P(None, None, "tensor"),
        P(None, "seq", "tensor"),
    )
    return jax.shard_map(
        body,
        mesh=mesh,
        in_specs=placed,
        out_specs=(P(None, "seq", "tensor"), P(None, None, "tensor"), P(None, "seq", "tensor")),
        check_vma=False,
    )
```

time: 1000 us -> 251 us (0.25)
  waiting for transfers between devices: 824 us -> 0.01 us
  Pallas kernels: 0 us -> 178 us
  blocking collectives: 44.2 us -> 0 us
  matrix products: 40.7 us -> 12.3 us
  local copies, waits for them, and re-layouts: 37 us -> 20.7 us
  between operations: 14.1 us -> 0.91 us
    psum x2 -> x0, waiting for transfers between devices: 605 us -> none  [the longest x1 562 us: body(): lax.psum(kernel_terms, 'seq') * position_scale]
    all_gather x2 -> x0, waiting for transfers between devices: 202 us -> none  [the longest x1 108 us: body(): lax.all_gather(keys, 'seq', axis=1, tiled=True)]
    pallas_call x0 -> x5, Pallas kernels: none -> 178 us  [the longest x2 61.8 us: tensor_sum(): pl.pallas_call(functools.partial(tensor_sum_kernel, has_base=base is not...]
    all_gather x2 -> x0, blocking collectives: 44.2 us -> none  [the longest x1 24.2 us: body(): full_in = lax.all_gather(tokens_in, 'tensor', axis=2, tiled=True)]
    dot_general x15 -> x5, matrix products: 40.7 us -> 12.3 us  [the longest x3 6.66 us: body(): jnp.dot(units, conv_weight[j], preferred_element_type=F32)]
    all_gather x2 -> x0, local copies, waits for them, and re-layouts: 22 us -> none  [the longest x1 15.6 us: body(): lax.all_gather(values_all, 'seq', axis=1, tiled=True)]
    unnamed x6 -> x0, waiting for transfers between devices: 14.8 us -> none
    convert_element_type x2 -> x7, local copies, waits for them, and re-layouts: 1.45 us -> 12.1 us  [the longest x2 4.66 us: body(): unit_normed, unit_inv = normalize(block_full.astype(F32))]
  transfers between devices with their start and end apart: 9 -> 4, of which waited for: 6 -> 0; matrix products, arithmetic and copies ran while one was open for 5% -> 11% of each run, Pallas kernels for 0% -> 59%
where the time goes in v1:
time: 251 us; the launch traced here: 250 us
  Pallas kernels  178 us (71%)
  other arithmetic  21.4 us (9%)
  local copies, waits for them, and re-layouts  20.7 us (8%)
  starting transfers between devices  16.4 us (7%)
  matrix products  12.3 us (5%)
    pallas_call x2, Pallas kernels, tensor_sum(): pl.pallas_call(functools.partial(tensor_sum_kernel, has_base=base is not...  61.8 us
    pallas_call x1, Pallas kernels, conv_grad_sum(): pl.pallas_call(conv_grad_kernel, name='conv_grad', out_shape=jax.ShapeDty...  51.5 us
    pallas_call x1, Pallas kernels, attention(): pl.pallas_call(attention_kernel, name='attention', out_shape=jax.ShapeDty...  40.9 us
    pallas_call x1, Pallas kernels, project(): pl.pallas_call(project_kernel, name='project', out_shape=(jax.ShapeDtypeS...  24 us
    ppermute x2, starting transfers between devices, from_neighbours(): after = lax.ppermute(head, axis, [(i + 1, i) for i in range(ends)])  10.7 us
    dot_general x3, matrix products, body(): jnp.dot(units, conv_weight[j], preferred_element_type=F32)  6.66 us
    ppermute x2, starting transfers between devices, from_neighbours(): before = lax.ppermute(tail, axis, [(i, i + 1) for i in range(ends)])  5.63 us
  transfers between devices with their start and end apart: 4, of which 0 were waited for; matrix products, arithmetic and copies ran while one was open for 11% of the time, Pallas kernels for 59%

profile of v1, /device:TPU:1, one launch (start us, length us, event | category | flops | bytes accessed | tf_op | source)
XLA Modules:
  0.0 249.8 jit_solution(11076544720985639784)
XLA Ops:
  0.6 0.0 copy-start
  0.6 1.7 fusion.39
  2.4 5.1 %collective-permute-start.2 = (bf16[2,64,384]{2,1,0:T(8,128)(2,1)}, bf16[2,64,384]{2,1,0:T(8,128)(2,1)}, u32[]{:S(2)}, u32[]{:S(2)}) collective-permute-start(bf16[2,64,384]{2,1,0:T(8,128)(2,1)} %get-tuple-element.21), channel_id=1, source_target_pairs={{4,0},{8,4},{12,8},{16,12},{20,16},{24,20},{28,24},{32,28},{36,32}... | collective-permute-start | bytes 294920 | tf_op jit(solution)/shard_map/ppermute | solution.py:596
  7.5 1.9 collective-permute-start.3
  9.4 24.0 %project.1 = (bf16[256,128]{1,0:T(8,128)(2,1)}, bf16[256,512]{1,0:T(8,128)(2,1)}) custom-call(bf16[256,384]{1,0:T(8,128)(2,1)} %bitcast.93, bf16[1536,128]{1,0:T(8,128)(2,1)} %wq_ref.1, bf16[1536,128]{1,0:T(8,128)(2,1)} %wk_ref.1, bf16[1536,384]{1,0:T(8,128)(2,1)} %wv_ref.1), custom_call_target="tpu_custom_call" | custom-call | tf_op jit(solution)/shard_map/project/pallas_call | solution.py:195
  33.4 40.9 %attention.1 = bf16[2,128,384]{2,1,0:T(8,128)(2,1)} custom-call(bf16[2,128,128]{2,1,0:T(8,128)(2,1)} %bitcast.102, bf16[2,128,512]{2,1,0:T(8,128)(2,1)} %bitcast.100), custom_call_target="tpu_custom_call" | custom-call | tf_op jit(solution)/shard_map/attention/pallas_call | solution.py:353
  74.3 0.0 copy-done
  74.3 1.5 convolution_convert_fusion
  75.8 0.3 copy.10
  76.1 1.2 copy.11
  77.3 31.0 %tensor_sum_4.1 = bf16[4,256,384]{2,1,0:T(8,128)(2,1)} custom-call(bf16[4,256,384]{2,1,0:T(8,128)(2,1)} %bitcast.85, bf16[256,384]{1,0:T(8,128)(2,1)} %bitcast.94), custom_call_target="tpu_custom_call" | custom-call | tf_op jit(solution)/shard_map/tensor_sum_4/pallas_call | solution.py:407
  108.2 0.0 copy-start.1
  108.3 1.4 convert_reduce_fusion
  109.6 1.2 convert_bitcast_fusion
  110.9 0.0 copy-done.1
  110.9 0.3 fusion.3
  111.3 1.6 copy.13
  112.9 3.0 %copy.14 = f32[256,1536]{1,0:T(8,128)} copy(f32[256,1536]{0,1:T(8,128)} %bitcast.83) | data formatting | bytes 3145728 | tf_op jit(solution)/shard_map/convert_element_type | solution.py:626
  115.9 2.9 %broadcast_multiply_fusion = (f32[256,1536]{1,0:T(8,128)}, f32[256,1536]{1,0:T(8,128)S(1)}) fusion(f32[256]{0:T(256)S(1)} %add_rsqrt_fusion, f32[256,1536]{1,0:T(8,128)} %copy.14, f32[256]{0:T(256)S(1)} %broadcast_multiply_fusion.3), kind=kLoop, calls=%fused_computation.40 | loop fusion | flops 1179648 | bytes 4720640 | tf_op jit(solution)/shard_map/mul | solution.py:40
  118.8 2.3 multiply_convert_fusion.1
  121.1 0.0 copy-start.3
  121.1 0.7 constant_dynamic-slice_fusion.1
  121.8 0.0 collective-permute-done.2
  121.8 0.0 collective-permute-done.3
  121.8 1.1 pad_maximum_fusion.2
  122.9 1.8 pad_maximum_fusion.cot_ref
  124.7 0.0 copy-done.3
  124.7 4.1 %fusion = bf16[256,1536]{1,0:T(8,128)(2,1)} fusion(bf16[3,1536,384]{2,1,0:T(8,128)(2,1)} %param.12, bf16[1,256,384]{2,1,0:T(8,128)(2,1)S(1)} %bitcast.98, bf16[1,256,384]{2,1,0:T(8,128)(2,1)S(1)} %bitcast.90, bf16[1,256,384]{2,1,0:T(8,128)(2,1)S(1)} %bitcast.96), kind=kOutput, calls=%fused_computation.2 | convolution fusion | flops 906952704 | bytes 4915200 | tf_op jit(solution)/shard_map/jrk,jck->rc/dot_general | solution.py:616
  128.8 2.3 copy.15
  131.1 2.3 copy.16
  133.4 30.8 %tensor_sum_3.1 = bf16[4,256,384]{2,1,0:T(8,128)(2,1)} custom-call(bf16[4,256,384]{2,1,0:T(8,128)(2,1)} %bitcast.88), custom_call_target="tpu_custom_call" | custom-call | tf_op jit(solution)/shard_map/tensor_sum_3/pallas_call | solution.py:407
  164.2 2.4 fusion.36
  166.6 0.6 copy.12
  167.2 1.2 convert_element_type.81
  168.4 0.0 copy-start.5
  168.4 2.1 fusion.19
  170.6 0.0 copy-done.5
  170.6 0.0 copy-start.2
  170.6 1.9 fusion.23
  172.5 0.0 copy-done.2
  172.5 1.2 convert_bitcast_fusion.1
  173.8 0.8 fusion.37
  174.6 5.6 %collective-permute-start.1 = (f32[2,64,384]{2,1,0:T(8,128)}, f32[2,64,384]{2,1,0:T(8,128)}, u32[]{:S(2)}, u32[]{:S(2)}) collective-permute-start(f32[2,64,384]{2,1,0:T(8,128)} %get-tuple-element.16), channel_id=1, source_target_pairs={{4,0},{8,4},{12,8},{16,12},{20,16},{24,20},{28,24},{32,28},{36,32}... | collective-permute-start | bytes 589832 | tf_op jit(solution)/shard_map/ppermute | solution.py:596
  180.2 0.8 fusion.38
  181.0 3.7 %collective-permute-start = (f32[2,64,384]{2,1,0:T(8,128)}, f32[2,64,384]{2,1,0:T(8,128)}, u32[]{:S(2)}, u32[]{:S(2)}) collective-permute-start(f32[2,64,384]{2,1,0:T(8,128)} %get-tuple-element.17), channel_id=1, source_target_pairs={{0,4},{4,8},{8,12},{12,16},{16,20},{20,24},{24,28},{28,32},{32,36}... | collective-permute-start | bytes 589832 | tf_op jit(solution)/shard_map/ppermute | solution.py:595
  184.7 3.0 %copy.17 = f32[256,4,384]{0,2,1:T(8,128)} copy(f32[256,4,384]{2,0,1:T(8,128)} %convert_bitcast_fusion.1) | data formatting | bytes 3145728 | tf_op jit(solution)/shard_map/convert_element_type | solution.py:643
  187.7 1.0 constant_dynamic-slice_fusion
  188.8 0.2 copy.19
  188.9 51.5 %conv_grad.1 = bf16[4608,384]{1,0:T(8,128)(2,1)} custom-call(bf16[256,1536]{1,0:T(8,128)(2,1)} %get-tuple-element.11.units_ref, bf16[3,256,384]{2,1,0:T(8,128)(2,1)} %pad_maximum_fusion.cot_ref), custom_call_target="tpu_custom_call" | custom-call | tf_op jit(solution)/shard_map/conv_grad/pallas_call | solution.py:570
  240.4 4.5 %multiply_convert_fusion = bf16[4608,384]{1,0:T(8,128)(2,1)} fusion(bf16[4608,384]{1,0:T(8,128)(2,1)} %conv_grad.1), kind=kLoop, calls=%fused_computation | loop fusion | flops 5308416 | bytes 7077888 | tf_op jit(solution)/shard_map/convert_element_type | solution.py:630
  244.9 0.0 copy-start.4
  244.9 0.0 copy-start.7
  244.9 0.0 copy-start.8
  244.9 0.0 copy-start.9
  244.9 1.5 fusion.29
  246.4 0.0 copy-done.4
  246.5 0.7 add_convert_fusion
  247.2 0.0 collective-permute-done.1
  247.2 0.0 collective-permute-done
  247.2 0.0 copy-done.6
  247.2 0.0 copy-done.7
  247.2 0.0 copy-done.8
  247.2 0.0 copy-done.9
  247.2 2.6 %fusion.35 = bf16[2,128,384]{2,1,0:T(8,128)(2,1)} fusion(f32[2,64,384]{2,1,0:T(8,128)S(1)} %copy-done.9, f32[2,64,384]{2,1,0:T(8,128)} %collective-permute-done, f32[2,64,384]{2,1,0:T(8,128)} %collective-permute-done.1, f32[2,64,384]{2,1,0:T(8,128)S(1)} %copy-done.8, bf16[2,128,384]{2,1,0:T(8,128)(2,1)S(1)} %bitcast.101, ...), kind=kOutput, calls=%fused_computation.53 | convolution fusion | flops 302678016 | bytes 3145728 | tf_op jit(solution)/shard_map/dot_general | solution.py:634
  (4 shorter events, 0.0 us)
Async XLA Ops:
  0.6 73.7 %copy-start = (bf16[384,1536]{1,0:T(8,128)(2,1)S(1)}, bf16[384,1536]{1,0:T(8,128)(2,1)}, u32[]{:S(2)}) copy-start(bf16[384,1536]{1,0:T(8,128)(2,1)} %param.11) | copy-start | bytes 3538948
  2.4 119.4 %collective-permute-start.2 = (bf16[2,64,384]{2,1,0:T(8,128)(2,1)}, bf16[2,64,384]{2,1,0:T(8,128)(2,1)}, u32[]{:S(2)}, u32[]{:S(2)}) collective-permute-start(bf16[2,64,384]{2,1,0:T(8,128)(2,1)} %get-tuple-element.21), channel_id=1, source_target_pairs={{4,0},{8,4},{12,8},{16,12},{20,16},{24,20},{28,24},{32,28},{36,32}... | collective-permute-start | bytes 294920 | tf_op jit(solution)/shard_map/ppermute | solution.py:596
  7.5 114.3 %collective-permute-start.3 = (bf16[2,64,384]{2,1,0:T(8,128)(2,1)}, bf16[2,64,384]{2,1,0:T(8,128)(2,1)}, u32[]{:S(2)}, u32[]{:S(2)}) collective-permute-start(bf16[2,64,384]{2,1,0:T(8,128)(2,1)} %get-tuple-element.22), channel_id=1, source_target_pairs={{0,4},{4,8},{8,12},{12,16},{16,20},{20,24},{24,28},{28,32},{32,36}... | collective-permute-start | bytes 294920 | tf_op jit(solution)/shard_map/ppermute | solution.py:595
  108.2 2.7 %copy-start.1 = (bf16[4,256,384]{2,1,0:T(8,128)(2,1)S(1)}, bf16[4,256,384]{2,1,0:T(8,128)(2,1)}, u32[]{:S(2)}) copy-start(bf16[4,256,384]{2,1,0:T(8,128)(2,1)} %tensor_sum_4.1) | copy-start | bytes 2359300
  121.1 3.6 %copy-start.3 = (bf16[2,128,384]{2,1,0:T(8,128)(2,1)S(1)}, bf16[2,128,384]{2,1,0:T(8,128)(2,1)}, u32[]{:S(2)}) copy-start(bf16[2,128,384]{2,1,0:T(8,128)(2,1)} %param.13) | copy-start | bytes 589828
  168.4 2.2 copy-start.5
  170.6 1.9 copy-start.2
  174.6 72.6 %collective-permute-start.1 = (f32[2,64,384]{2,1,0:T(8,128)}, f32[2,64,384]{2,1,0:T(8,128)}, u32[]{:S(2)}, u32[]{:S(2)}) collective-permute-start(f32[2,64,384]{2,1,0:T(8,128)} %get-tuple-element.16), channel_id=1, source_target_pairs={{4,0},{8,4},{12,8},{16,12},{20,16},{24,20},{28,24},{32,28},{36,32}... | collective-permute-start | bytes 589832 | tf_op jit(solution)/shard_map/ppermute | solution.py:596
  181.0 66.2 %collective-permute-start = (f32[2,64,384]{2,1,0:T(8,128)}, f32[2,64,384]{2,1,0:T(8,128)}, u32[]{:S(2)}, u32[]{:S(2)}) collective-permute-start(f32[2,64,384]{2,1,0:T(8,128)} %get-tuple-element.17), channel_id=1, source_target_pairs={{0,4},{4,8},{8,12},{12,16},{16,20},{20,24},{24,28},{28,32},{32,36}... | collective-permute-start | bytes 589832 | tf_op jit(solution)/shard_map/ppermute | solution.py:595
  244.9 1.6 copy-start.4
  244.9 2.3 copy-start.6
  244.9 2.3 copy-start.7
  244.9 2.3 copy-start.8
  244.9 2.3 copy-start.9

commit v2 on v1

--- a/solution.py
+++ b/solution.py
@@ -22,7 +22,7 @@
 F32 = jnp.float32
 VMEM = pltpu.VMEM
 VSPEC = pl.BlockSpec(memory_space=pltpu.VMEM)
-VMEM_LIMIT = 60 * 1024 * 1024
+HSPEC = pl.BlockSpec(memory_space=pltpu.HBM)
 
 
 def normalize(values):
@@ -159,65 +159,137 @@
     return t, {"tensor": nxt(t, 1)}, {"tensor": nxt(t, 3)}
 
 
-def params(cid):
+def params(cid, mib):
     return pltpu.CompilerParams(
-        collective_id=cid, has_side_effects=True, vmem_limit_bytes=VMEM_LIMIT
-    )
-
-
-def project_kernel(tok_ref, wq_ref, wk_ref, wv_ref, q_ref, kv_ref, full, ss, rs):
+        collective_id=cid, has_side_effects=True, vmem_limit_bytes=mib * 1024 * 1024
+    )
+
+
+def seq_next(k):
+    return {"seq": lax.rem(lax.axis_index("seq") + k, NX * NY * NZ * NC)}
+
+
+def seq_prev():
+    return seq_next(NX * NY * NZ * NC - 1)
+
+
+def fetch(sem, i, src, dst):
+    c = pltpu.make_async_copy(src, dst, sem.at[i])
+    c.start()
+    return c
+
+
+def project_kernel(
+    tok_ref, cot_ref, wq_hbm, wk_hbm, wv_hbm, cw_hbm,
+    q_ref, kv_ref, cotx, terms_ref,
+    full, wq, wk, wv, cw, cots, ss, rs, ls,
+):
     t, plus, minus = tensor_ring()
     rows, width = tok_ref.shape
     half = rows // 2
-    greet([plus, minus])
+    edge = CONV_DILATION
+    count = cot_ref.shape[1]
+    me = lax.axis_index("seq")
+    last = NX * NY * NZ * NC - 1
+    ccw = fetch(ls, 0, cw_hbm, cw)
+    cw3 = [fetch(ls, 1, wq_hbm, wq), fetch(ls, 2, wk_hbm, wk), fetch(ls, 3, wv_hbm, wv)]
+    full[t] = tok_ref[...]
+    cotx[:, edge : edge + count] = cot_ref[...]
+    greet([plus, minus, seq_next(1), seq_prev()])
 
     def view(slot, h):
         return full.at[slot, pl.ds(h * half, half)]
 
-    full[t] = tok_ref[...]
     s = Sender(ss, rs)
     g = Gather4(s, view, t, plus, minus)
     g.begin()
+    up = s.go(cot_ref.at[:, count - edge : count], cotx.at[:, 0:edge], seq_next(1))
+    down = s.go(cot_ref.at[:, 0:edge], cotx.at[:, edge + count : 2 * edge + count], seq_prev())
+    up.wait_recv()
+    down.wait_recv()
+
+    @pl.when(me == 0)
+    def _():
+        cotx[:, 0:edge] = jnp.zeros((2, edge, width), BF)
+
+    @pl.when(me == last)
+    def _():
+        cotx[:, edge + count : 2 * edge + count] = jnp.zeros((2, edge, width), BF)
+
+    for j in range(3):
+        cots[j] = cotx[:, (2 - j) * edge : (2 - j) * edge + count].reshape(rows, width)
+    ccw.wait()
+
+    def term(p):
+        acc = jnp.zeros((rows, width), F32)
+        for j in range(3):
+            acc = acc + lax.dot_general(
+                cots[j],
+                cw[j, p * width : (p + 1) * width],
+                (((1,), (1,)), ((), ())),
+                preferred_element_type=F32,
+            )
+        terms_ref[p] = acc.astype(BF)
+
+    term(0)
     g.relay()
+    for p in range(1, NT):
+        term(p)
+    for c in cw3:
+        c.wait()
     g.wait_near()
     g.wait_far()
-    values = jnp.concatenate([full[i] for i in range(NT)], axis=1).astype(F32)
-    hidden = normalize(values)[0].astype(BF)
-    q_ref[...] = jnp.dot(hidden, wq_ref[...], preferred_element_type=F32).astype(BF)
-    keys = q_ref.shape[1]
-    kv_ref[:, :keys] = jnp.dot(hidden, wk_ref[...], preferred_element_type=F32).astype(BF)
-    kv_ref[:, keys:] = jnp.dot(hidden, wv_ref[...], preferred_element_type=F32).astype(BF)
+    for h in range(2):
+        at = slice(h * half, (h + 1) * half)
+        values = jnp.concatenate([full[i, at] for i in range(NT)], axis=1).astype(F32)
+        hidden = normalize(values)[0].astype(BF)
+        q_ref[h] = jnp.dot(hidden, wq[...], preferred_element_type=F32).astype(BF)
+        keys = q_ref.shape[2]
+        kv_ref[h, :, :keys] = jnp.dot(hidden, wk[...], preferred_element_type=F32).astype(BF)
+        kv_ref[h, :, keys:] = jnp.dot(hidden, wv[...], preferred_element_type=F32).astype(BF)
     s.drain()
 
 
-def project(tokens, wq, wk, wv):
+def project(tokens, cot, wq, wk, wv, cw):
     rows, width = tokens.shape
+    seqs, count, _ = cot.shape
     return pl.pallas_call(
         project_kernel,
         name="project",
         out_shape=(
-            jax.ShapeDtypeStruct((rows, wq.shape[1]), BF),
-            jax.ShapeDtypeStruct((rows, wk.shape[1] + wv.shape[1]), BF),
+            jax.ShapeDtypeStruct((seqs, count, wq.shape[1]), BF),
+            jax.ShapeDtypeStruct((seqs, count, wk.shape[1] + wv.shape[1]), BF),
+            jax.ShapeDtypeStruct((seqs, count + 2 * CONV_DILATION, width), BF),
+            jax.ShapeDtypeStruct((NT, rows, width), BF),
         ),
-        in_specs=[VSPEC] * 4,
-        out_specs=(VSPEC, VSPEC),
+        in_specs=[VSPEC] * 2 + [HSPEC] * 4,
+        out_specs=(VSPEC,) * 4,
         scratch_shapes=[
             VMEM((NT, rows, width), BF),
-            pltpu.SemaphoreType.DMA((6,)),
-            pltpu.SemaphoreType.DMA((6,)),
+            VMEM(wq.shape, BF),
+            VMEM(wk.shape, BF),
+            VMEM(wv.shape, BF),
+            VMEM(cw.shape, BF),
+            VMEM((3, rows, width), BF),
+            pltpu.SemaphoreType.DMA((8,)),
+            pltpu.SemaphoreType.DMA((8,)),
+            pltpu.SemaphoreType.DMA((4,)),
         ],
-        compiler_params=params(1),
-    )(tokens, wq, wk, wv)
-
-
-def attention_kernel(q_ref, kv_ref, out_ref, qbuf, kvbuf, obuf, orecv, lbuf, lrecv, ss, rs):
+        compiler_params=params(1, 32),
+    )(tokens, cot, wq, wk, wv, cw)
+
+
+def attention_kernel(
+    q_ref, kv_ref, terms_ref, out_ref, ug_ref, rbuf, qbuf, kvbuf, obuf, orecv, lbuf, lrecv, ss, rs
+):
     x, y, z, core = seq_pos()
+    t, plus, minus = tensor_ring()
     count = q_ref.shape[1]
     partner = {"seq": seq_dev(x, y, z, 1 - core)}
     zpeer = {"seq": seq_dev(x, y, 1 - z, core)}
     xs = [{"seq": seq_dev(nxt(x, k), y, z, core)} for k in (1, 2, 3)]
     ys = [{"seq": seq_dev(x, nxt(y, k), z, core)} for k in (1, 2, 3)]
-    greet([partner, zpeer] + xs + ys)
+    greet([partner, zpeer, plus, minus] + xs + ys)
     s = Sender(ss, rs)
     half = count // 2
     axes = ((x, xs, y, ys), (y, ys, x, xs))
@@ -246,6 +318,12 @@
         gk.begin()
         fw = [s.go(own, own, partner)]
         state.append((cz, gk, go, gq, fw))
+
+    def term(p, h):
+        return terms_ref.at[p, pl.ds(h * count, count)]
+
+    red = Reduce4(s, term, lambda i, h: rbuf.at[i], t, plus, minus)
+    red.begin()
     for i, (a, a_dev, b, b_dev) in enumerate(axes):
         cz, gk, go, gq, fw = state[i]
         cz.wait_recv()
@@ -275,6 +353,7 @@
         fw.append(s.go(ref, ref, partner))
         gq.wait_near()
         gq.wait_far()
+    red.combine()
     lane = lax.broadcasted_iota(jnp.int32, (count, 128), 1)
     scale = KEY ** (-0.5)
     keys = NX * NZ * NC * count
@@ -317,6 +396,9 @@
             sent.append(s.go(lbuf.at[i, nxt(b, k)], lrecv.at[i, b], dev))
         orecv[i, b] = obuf[i, b]
         lrecv[i, b] = lbuf[i, b]
+    parts = red.finish()
+    for h in range(2):
+        ug_ref[h * count : (h + 1) * count] = parts[h]
     for c in sent:
         c.wait_recv()
     for i in range(2):
@@ -346,17 +428,21 @@
     s.drain()
 
 
-def attention(q, kv):
+def attention(q, kv, terms):
     seqs, count, keys = q.shape
     vals = kv.shape[2] - keys
-    n = 2 * (1 + 6 * 3 + 8 + 6)
+    n = 2 * (1 + 6 * 3 + 8 + 6) + 6
     return pl.pallas_call(
         attention_kernel,
         name="attention",
-        out_shape=jax.ShapeDtypeStruct((seqs, count, vals), BF),
-        in_specs=[VSPEC] * 2,
-        out_specs=VSPEC,
+        out_shape=(
+            jax.ShapeDtypeStruct((seqs, count, vals), BF),
+            jax.ShapeDtypeStruct(terms.shape[1:], F32),
+        ),
+        in_specs=[VSPEC] * 3,
+        out_specs=(VSPEC, VSPEC),
         scratch_shapes=[
+            VMEM((8, count, terms.shape[2]), BF),
             VMEM((seqs, 4, count, keys), BF),
             VMEM((seqs, 4, NZ, NC, count, keys + vals), BF),
             VMEM((seqs, 4, count, vals), BF),
@@ -366,64 +452,24 @@
             pltpu.SemaphoreType.DMA((n,)),
             pltpu.SemaphoreType.DMA((n,)),
         ],
-        compiler_params=params(2),
-    )(q, kv)
-
-
-def tensor_sum_kernel(terms_ref, *refs, has_base):
-    if has_base:
-        base_ref, out_ref, rbuf, ss, rs = refs
-    else:
-        out_ref, rbuf, ss, rs = refs
-    t, plus, minus = tensor_ring()
-    rows = terms_ref.shape[1]
-    half = rows // 2
-    greet([plus, minus])
-    s = Sender(ss, rs)
-
-    def x(p, h):
-        return terms_ref.at[p, pl.ds(h * half, half)]
-
-    red = Reduce4(s, x, lambda i, h: rbuf.at[i], t, plus, minus)
-    red.begin()
-    red.combine()
-    parts = red.finish()
-    for h in range(2):
-        part = parts[h]
-        if has_base:
-            part = part + base_ref[h * half : (h + 1) * half].astype(F32)
-        out_ref[t, pl.ds(h * half, half)] = part.astype(BF)
-    g = Gather4(s, lambda p, h: out_ref.at[p, pl.ds(h * half, half)], t, plus, minus)
-    g.begin()
-    g.relay()
-    g.wait_near()
-    g.wait_far()
-    s.drain()
-
-
-def tensor_sum(terms, base, cid):
-    _, rows, width = terms.shape
-    args = (terms,) if base is None else (terms, base)
-    return pl.pallas_call(
-        functools.partial(tensor_sum_kernel, has_base=base is not None),
-        name="tensor_sum_%d" % cid,
-        out_shape=jax.ShapeDtypeStruct(terms.shape, BF),
-        in_specs=[VSPEC] * len(args),
-        out_specs=VSPEC,
-        scratch_shapes=[
-            VMEM((8, rows // 2, width), BF),
-            pltpu.SemaphoreType.DMA((12,)),
-            pltpu.SemaphoreType.DMA((12,)),
-        ],
-        compiler_params=params(cid),
-    )(*args)
-
-
-def conv_grad_kernel(
-    units_ref, cot_ref, out_ref, send, recv, sums, r1, mid, r2, fin, zrecv, ss, rs
+        compiler_params=params(2, 40),
+    )(q, kv, terms)
+
+
+def tail_kernel(
+    att_ref, tok_ref, cotx, ug_ref, ow, cw,
+    block_out, out_ref, residual,
+    terms, rt, blk, units, cots, taps, halo, st,
+    send, recv, sums, r1, mid, r2, fin, zrecv, ss, rs,
 ):
     x, y, z, core = seq_pos()
-    width = units_ref.shape[1]
+    t, plus, minus = tensor_ring()
+    me = lax.axis_index("seq")
+    last = NX * NY * NZ * NC - 1
+    rows, local = att_ref.shape
+    half = rows // 2
+    width = NT * local
+    edge = CONV_DILATION
     total = 3 * width
     mine = total // 2
     tile = 256
@@ -444,14 +490,56 @@
     partner = {"seq": seq_dev(x, y, z, 1 - core)}
     zpeer = {"seq": seq_dev(x, y, 1 - z, core)}
     ap, am, bp, bm = along_a(1), along_a(3), along_b(1), along_b(3)
-    greet([partner, zpeer, ap, am, bp, bm])
-
-    def product(g):
-        tap = lax.div(g, per_tap)
-        col = pl.multiple_of(lax.rem(g, per_tap) * tile, tile)
+    opposite = {"tensor": nxt(t, 2)}
+    after, before = seq_next(1), seq_prev()
+    greet([plus, minus, opposite, partner, zpeer, ap, am, bp, bm, after, before])
+
+    s = Sender(ss, rs)
+    s.n = tiles
+
+    def term(p, h):
+        return terms.at[p, pl.ds(h * half, half)]
+
+    def project_to(p):
+        col = pl.multiple_of(p * local, 128)
+        terms[p] = jnp.dot(
+            att_ref[...], ow[:, pl.ds(col, local)], preferred_element_type=F32
+        ).astype(BF)
+
+    for k in (2, 1, 3, 0):
+        project_to(nxt(t, k))
+    red = Reduce4(s, term, lambda i, h: rt.at[i], t, plus, minus)
+    red.begin()
+    for j in range(3):
+        cots[j] = cotx[:, (2 - j) * edge : (2 - j) * edge + half].reshape(rows, local)
+    red.combine()
+    parts = red.finish()
+    for h in range(2):
+        base = tok_ref[h * half : (h + 1) * half].astype(F32)
+        blk[t, pl.ds(h * half, half)] = (parts[h] + base).astype(BF)
+    g = Gather4(s, lambda p, h: blk.at[p, pl.ds(h * half, half)], t, plus, minus)
+    g.begin()
+    g.relay()
+    g.wait_near()
+    g.wait_far()
+
+    averages, invs = [], []
+    for h in range(2):
+        at = slice(h * half, (h + 1) * half)
+        values = jnp.concatenate([blk[i, at] for i in range(NT)], axis=1).astype(F32)
+        average = jnp.mean(values, axis=-1, keepdims=True)
+        centred = values - average
+        inv = lax.rsqrt(jnp.mean(centred * centred, axis=-1, keepdims=True) + eps_norm)
+        units[at] = gelu_exact(centred * inv).astype(BF)
+        averages.append(average)
+        invs.append(inv)
+
+    def product(q):
+        tap = lax.div(q, per_tap)
+        col = pl.multiple_of(lax.rem(q, per_tap) * tile, tile)
         return lax.dot_general(
-            units_ref[:, pl.ds(col, tile)],
-            cot_ref[tap],
+            units[:, pl.ds(col, tile)],
+            cots[tap],
             (((0,), (0,)), ((), ())),
             preferred_element_type=F32,
         )
@@ -478,8 +566,6 @@
         row = pl.multiple_of(i * tile, tile)
         sums[pl.ds(row, tile)] = (own + recv[i].astype(F32)).astype(BF)
 
-    s = Sender(ss, rs)
-    s.n = tiles
     big = mine // 4
     small = big // 4
     bh = (0, big // 2)
@@ -500,7 +586,27 @@
         am,
     )
     first.begin()
+
+
+    def tap(j):
+        return jnp.dot(units[...], cw[j], preferred_element_type=F32).reshape(2, half, local)
+
+    taps[0] = tap(0)
+    up = s.go(taps.at[0, :, half - edge : half], halo.at[0], after)
+    taps[2] = tap(2)
+    down = s.go(taps.at[2, :, 0:edge], halo.at[1], before)
+    lane = lax.broadcasted_iota(jnp.int32, (half, 128), 1)
+    for h in range(2):
+        at = pl.ds(h * half, half)
+        n = (blk[t, at].astype(F32) - averages[h]) * invs[h]
+        slope = ug_ref[h * half : (h + 1) * half] * gelu_slope(n)
+        one = jnp.sum(slope, axis=-1, keepdims=True)
+        two = jnp.sum(slope * n, axis=-1, keepdims=True)
+        stats = jnp.where(lane == 0, one, jnp.where(lane == 1, two, 0.0))
+        st[t, h] = stats.T[0:8]
+    stat_copies = [s.go(st.at[t], st.at[t], d) for d in (plus, minus, opposite)]
     first.combine()
+    taps[1] = tap(1)
     h0, h1 = first.finish()
     mid[0 : big // 2] = h0.astype(BF)
     mid[big // 2 : big] = h1.astype(BF)
@@ -513,14 +619,27 @@
         bm,
     )
     second.begin()
+    up.wait_recv()
+    down.wait_recv()
     second.combine()
     h0, h1 = second.finish()
     fin[0:cut] = h0.astype(BF)
     fin[cut:small] = h1.astype(BF)
     cz = s.go(fin, zrecv, zpeer)
+
+    for h in range(2):
+        own = blk[t, pl.ds(h * half, half)].astype(F32) + taps[1, h]
+        left = jnp.where(me == 0, 0.0, halo[0, h])
+        right = jnp.where(me == last, 0.0, halo[1, h])
+        block_out[h, 0:edge] = (own[:edge] + left + taps[2, h, edge:half]).astype(BF)
+        block_out[h, edge:half] = (own[edge:] + taps[0, h, 0 : half - edge] + right).astype(BF)
+
     cz.wait_recv()
+    scale = (rows * NX * NY * NZ * NC) ** (-0.5)
     at = core * mine + a * big + b * small
-    out_ref[pl.ds(m16(at), small)] = (fin[...].astype(F32) + zrecv[...].astype(F32)).astype(BF)
+    out_ref[pl.ds(m16(at), small)] = (
+        (fin[...].astype(F32) + zrecv[...].astype(F32)) * scale
+    ).astype(BF)
     g2 = Gather4(
         s,
         lambda p, h: out_ref.at[pl.ds(m16(core * mine + a * big + p * small + sh[h]), sn[h])],
@@ -545,6 +664,16 @@
     )
     g1.begin()
     fw = [s.go(block(a), block(a), partner)]
+    for c in stat_copies:
+        c.wait_recv()
+    for h in range(2):
+        at = pl.ds(h * half, half)
+        n = (blk[t, at].astype(F32) - averages[h]) * invs[h]
+        slope = ug_ref[h * half : (h + 1) * half] * gelu_slope(n)
+        both = (st[0, h] + st[1, h] + st[2, h] + st[3, h]) * (1.0 / width)
+        wide = jnp.concatenate([both, jnp.zeros((120, 128), F32)], axis=0).T
+        grad = (slope - wide[:, 0:1] - n * wide[:, 1:2]) * invs[h]
+        residual[h] = (cotx[h, edge : edge + half].astype(F32) + grad).astype(BF)
     g1.relay()
     g1.wait_near()
     for k in (1, 3):
@@ -560,20 +689,34 @@
         exchange(i).wait_send()
 
 
-def conv_grad_sum(units, cots):
-    rows, width = units.shape
-    local = cots.shape[2]
+def tail(attended, tokens, cotx, unit_grad, out_weight, conv_weight):
+    rows, local = attended.shape
+    width = local * NT
+    half = rows // 2
+    edge = CONV_DILATION
     mine = 3 * width // 2
     big, small = mine // 4, mine // 16
     cut = (small // 2 + 15) // 16 * 16
-    n = mine // 256 + 6 * 4 + 1 + 4
+    n = mine // 256 + 6 * 6 + 1 + 4 + 2 + 3
     return pl.pallas_call(
-        conv_grad_kernel,
-        name="conv_grad",
-        out_shape=jax.ShapeDtypeStruct((3 * width, local), BF),
-        in_specs=[VSPEC] * 2,
-        out_specs=VSPEC,
+        tail_kernel,
+        name="tail",
+        out_shape=(
+            jax.ShapeDtypeStruct((2, half, local), BF),
+            jax.ShapeDtypeStruct((3 * width, local), BF),
+            jax.ShapeDtypeStruct((2, half, local), BF),
+        ),
+        in_specs=[VSPEC] * 6,
+        out_specs=(VSPEC,) * 3,
         scratch_shapes=[
+            VMEM((NT, rows, local), BF),
+            VMEM((8, half, local), BF),
+            VMEM((NT, rows, local), BF),
+            VMEM((rows, width), BF),
+            VMEM((3, rows, local), BF),
+            VMEM((3, 2, half, local), F32),
+            VMEM((2, 2, edge, local), F32),
+            VMEM((NT, 2, 8, 128), F32),
             VMEM((mine // 256, 256, local), BF),
             VMEM((mine // 256, 256, local), BF),
             VMEM((mine, local), BF),
@@ -585,69 +728,22 @@
             pltpu.SemaphoreType.DMA((n,)),
             pltpu.SemaphoreType.DMA((n,)),
         ],
-        compiler_params=params(5),
-    )(units, cots)
-
-
-def from_neighbours(head, tail, axis):
-    count = lax.axis_size(axis)
-    ends = count - 1
-    before = lax.ppermute(tail, axis, [(i, i + 1) for i in range(ends)])
-    after = lax.ppermute(head, axis, [(i + 1, i) for i in range(ends)])
-    return before, after
+        compiler_params=params(3, 40),
+    )(attended, tokens, cotx, unit_grad, out_weight, conv_weight)
 
 
 def body(tokens_in, query_weight, key_weight, value_weight, out_weight, conv_weight, cotangent):
     seqs, count, local = tokens_in.shape
-    width = local * NT
     rows = seqs * count
-    edge = CONV_DILATION
-    q, kv = project(tokens_in.reshape(rows, local), query_weight, key_weight, value_weight)
-    attended = attention(q.reshape(seqs, count, -1), kv.reshape(seqs, count, -1))
-
-    before, after = from_neighbours(cotangent[:, :edge], cotangent[:, count - edge :], "seq")
-    cot_ext = jnp.concatenate([before, cotangent, after], axis=1)
-    cots = jnp.stack(
-        [
-            cot_ext[:, (2 - j) * edge : (2 - j) * edge + count].reshape(rows, local)
-            for j in range(3)
-        ]
-    )
-    unit_terms = jnp.einsum("jrk,jck->rc", cots, conv_weight, preferred_element_type=F32)
-    unit_terms = unit_terms.astype(BF).reshape(rows, NT, local).transpose(1, 0, 2)
-    unit_grad = tensor_sum(unit_terms, None, 3)
-
-    mixed = jnp.dot(attended.reshape(rows, local), out_weight, preferred_element_type=F32)
-    mixed = mixed.astype(BF).reshape(rows, NT, local).transpose(1, 0, 2)
-    block_full = tensor_sum(mixed, tokens_in.reshape(rows, local), 4)
-    t = lax.axis_index("tensor")
-    block_in = lax.dynamic_index_in_dim(block_full, t, 0, keepdims=False)
-    block_full = block_full.transpose(1, 0, 2).reshape(rows, width)
-    unit_normed, unit_inv = normalize(block_full.astype(F32))
-    units = gelu_exact(unit_normed).astype(BF)
-
-    conv_grad = conv_grad_sum(units, cots)
-    conv_grad = (conv_grad.astype(F32) * ((rows * lax.axis_size("seq")) ** (-0.5))).astype(BF)
-    conv_grad = conv_grad.reshape(3, width, local)
-
-    taps = [
-        jnp.dot(units, conv_weight[j], preferred_element_type=F32).reshape(seqs, count, local)
-        for j in range(3)
-    ]
-    before, after = from_neighbours(taps[2][:, :edge], taps[0][:, count - edge :], "seq")
-    from_left = jnp.concatenate([before, taps[0][:, : count - edge]], axis=1)
-    from_right = jnp.concatenate([taps[2][:, edge:], after], axis=1)
-    conv_out = from_left + taps[1] + from_right
-    block_out = (block_in.reshape(seqs, count, local).astype(F32) + conv_out).astype(BF)
-
-    unit_grad = unit_grad.transpose(1, 0, 2).reshape(rows, width).astype(F32)
-    slope_grad = unit_grad * gelu_slope(unit_normed)
-    first_mean = jnp.sum(slope_grad, axis=-1, keepdims=True) / width
-    second_mean = jnp.sum(slope_grad * unit_normed, axis=-1, keepdims=True) / width
-    full_grad = (slope_grad - first_mean - unit_normed * second_mean) * unit_inv
-    input_grad = lax.dynamic_slice_in_dim(full_grad, t * local, local, 1)
-    residual_grad = (cotangent.astype(F32) + input_grad.reshape(seqs, count, local)).astype(BF)
-    return (block_out, conv_grad, residual_grad)
+    tokens = tokens_in.reshape(rows, local)
+    q, kv, cotx, terms = project(
+        tokens, cotangent, query_weight, key_weight, value_weight, conv_weight
+    )
+    attended, unit_grad = attention(q, kv, terms)
+    block_out, conv_grad, residual_grad = tail(
+        attended.reshape(rows, local), tokens, cotx, unit_grad, out_weight, conv_weight
+    )
+    return (block_out, conv_grad.reshape(3, local * NT, local), residual_grad)
 
 
 def solution(mesh):

time: 251 us -> 166 us (0.66)
  Pallas kernels: 178 us -> 155 us
  other arithmetic: 21.4 us -> 0 us
  starting transfers between devices: 16.4 us -> 0 us
  matrix products: 12.3 us -> 0 us
  local copies, waits for them, and re-layouts: 20.7 us -> 10.3 us
    pallas_call x4 -> x2, Pallas kernels: 154 us -> 126 us  [the longest x1 84.1 us: tail(): pl.pallas_call(tail_kernel, name='tail', out_shape=(jax.ShapeDtypeStruct(...]
    ppermute x4 -> x0, starting transfers between devices: 16.4 us -> none  [the longest x2 10.7 us: from_neighbours(): after = lax.ppermute(head, axis, [(i + 1, i) for i in range(ends)])]
    dot_general x5 -> x0, matrix products: 12.3 us -> none  [the longest x3 6.66 us: body(): jnp.dot(units, conv_weight[j], preferred_element_type=F32)]
    convert_element_type x7 -> x0, local copies, waits for them, and re-layouts: 12.1 us -> none  [the longest x2 4.66 us: body(): unit_normed, unit_inv = normalize(block_full.astype(F32))]
    unnamed x21, local copies, waits for them, and re-layouts: 0.21 us -> 10.3 us
    convert_element_type x5 -> x0, other arithmetic: 9.93 us -> none  [the longest x1 4.47 us: body(): (conv_grad.astype(F32) * (rows * lax.axis_size('seq')) ** (-0.5)).astype(BF)]
    pallas_call x1, Pallas kernels: 24 us -> 28.9 us  [project(): pl.pallas_call(project_kernel, name='project', out_shape=(jax.ShapeDtypeS...]
    mul x2 -> x0, other arithmetic: 4.41 us -> none  [the longest x1 2.88 us: gelu_slope(): values * inv_root_two_pi * jnp.exp(-0.5 * values * values)]
  transfers between devices with their start and end apart: 4 -> 0, of which waited for: 0 -> 0; matrix products, arithmetic and copies ran while one was open for 11% -> 0% of each run, Pallas kernels for 59% -> 0%
where the time goes in v2:
time: 166 us
  Pallas kernels  155 us (93%)
  local copies, waits for them, and re-layouts  10.3 us (6%)
    pallas_call x1, Pallas kernels, tail(): pl.pallas_call(tail_kernel, name='tail', out_shape=(jax.ShapeDtypeStruct(...  84.1 us
    pallas_call x1, Pallas kernels, attention(): pl.pallas_call(attention_kernel, name='attention', out_shape=(jax.ShapeDt...  41.8 us
    pallas_call x1, Pallas kernels, project(): pl.pallas_call(project_kernel, name='project', out_shape=(jax.ShapeDtypeS...  28.9 us
    unnamed x21, local copies, waits for them, and re-layouts  10.3 us

profile of v2, /device:TPU:1, one launch (start us, length us, event | category | flops | bytes accessed | tf_op | source)
XLA Modules:
  0.0 165.8 jit_solution(2702482904125183896)
XLA Ops:
  0.6 0.0 copy-start
  0.6 2.0 %copy-done = bf16[3,1536,384]{2,1,0:T(8,128)(2,1)S(1)} copy-done((bf16[3,1536,384]{2,1,0:T(8,128)(2,1)S(1)}, bf16[3,1536,384]{2,1,0:T(8,128)(2,1)}, u32[]{:S(2)}) %copy-start) | copy-done | bytes 3538968
  2.6 0.0 copy-start.2
  2.6 1.3 copy-done.2
  3.9 0.0 copy-start.4
  3.9 0.9 copy-done.4
  4.8 0.0 copy-start.6
  4.8 1.0 copy-done.6
  5.8 0.0 copy-start.7
  5.8 1.0 copy-done.7
  6.8 0.0 copy-start.8
  6.8 0.9 copy-done.8
  7.8 0.0 copy-start.1
  7.8 0.0 copy-start.3
  7.8 0.0 copy-start.5
  7.8 28.9 %project.1 = (bf16[2,128,128]{2,1,0:T(8,128)(2,1)S(1)}, bf16[2,128,512]{2,1,0:T(8,128)(2,1)S(1)}, bf16[2,256,384]{2,1,0:T(8,128)(2,1)S(1)}, bf16[4,256,384]{2,1,0:T(8,128)(2,1)S(1)}) custom-call(bf16[256,384]{1,0:T(8,128)(2,1)S(1)} %bitcast.4, bf16[2,128,384]{2,1,0:T(8,128)(2,1)S(1)} %copy-done.8, bf16[1536,128]{1,0:T(8,128)(2,1)S(1)} %copy-done.6, ...), custom_call_target="tpu_custom_call" | custom-call | tf_op jit(solution)/shard_map/project/pallas_call | solution.py:256
  36.7 41.8 %attention.1 = (bf16[2,128,384]{2,1,0:T(8,128)(2,1)S(1)}, f32[256,384]{1,0:T(8,128)S(1)}) custom-call(bf16[2,128,128]{2,1,0:T(8,128)(2,1)S(1)} %get-tuple-element.12.q_ref, bf16[2,128,512]{2,1,0:T(8,128)(2,1)S(1)} %get-tuple-element.13.kv_ref, bf16[4,256,384]{2,1,0:T(8,128)(2,1)S(1)} %get-tuple-element.14.terms_ref), custom_call_target="tpu_custom_call" | custom-call | tf_op jit(solution)/shard_map/attention/pallas_call | solution.py:435
  78.5 0.0 copy-done.1
  78.5 0.0 copy-done.3
  78.5 0.0 copy-done.5
  78.5 84.1 %tail.1 = (bf16[2,128,384]{2,1,0:T(8,128)(2,1)S(1)}, bf16[4608,384]{1,0:T(8,128)(2,1)S(1)}, bf16[2,128,384]{2,1,0:T(8,128)(2,1)S(1)}) custom-call(bf16[256,384]{1,0:T(8,128)(2,1)S(1)} %bitcast.6, bf16[256,384]{1,0:T(8,128)(2,1)S(1)} %bitcast.5, bf16[2,256,384]{2,1,0:T(8,128)(2,1)S(1)} %get-tuple-element.16.cotx, f32[256,384]{1,0:T(8,128)S(1)} %get-tuple-element.17.ug_ref, ...), custom_call_target="tpu_custom_call" | custom-call | tf_op jit(solution)/shard_map/tail/pallas_call | solution.py:701
  162.7 0.7 copy.13
  163.4 1.8 %copy.14 = bf16[3,1536,384]{2,1,0:T(8,128)(2,1)} copy(bf16[3,1536,384]{2,1,0:T(8,128)(2,1)S(1)} %bitcast.3) | data formatting | bytes 7077888
  165.1 0.7 copy.15
Async XLA Ops:
  0.6 2.0 %copy-start = (bf16[3,1536,384]{2,1,0:T(8,128)(2,1)S(1)}, bf16[3,1536,384]{2,1,0:T(8,128)(2,1)}, u32[]{:S(2)}) copy-start(bf16[3,1536,384]{2,1,0:T(8,128)(2,1)} %cw.1) | copy-start | bytes 10616836
  2.6 1.3 copy-start.2
  3.9 0.9 copy-start.4
  4.8 1.0 copy-start.6
  5.8 1.0 copy-start.7
  6.8 0.9 copy-start.8
  7.8 70.8 %copy-start.1 = (bf16[3,1536,384]{2,1,0:T(8,128)(2,1)S(1)}, bf16[3,1536,384]{2,1,0:T(8,128)(2,1)}, u32[]{:S(2)}) copy-start(bf16[3,1536,384]{2,1,0:T(8,128)(2,1)} %cw.1) | copy-start | bytes 10616836
  7.8 70.8 %copy-start.3 = (bf16[384,1536]{1,0:T(8,128)(2,1)S(1)}, bf16[384,1536]{1,0:T(8,128)(2,1)}, u32[]{:S(2)}) copy-start(bf16[384,1536]{1,0:T(8,128)(2,1)} %ow.1) | copy-start | bytes 3538948
  7.8 70.8 %copy-start.5 = (bf16[2,128,384]{2,1,0:T(8,128)(2,1)S(1)}, bf16[2,128,384]{2,1,0:T(8,128)(2,1)}, u32[]{:S(2)}) copy-start(bf16[2,128,384]{2,1,0:T(8,128)(2,1)} %param.7) | copy-start | bytes 589828

commit v3 on v2

v3 whole, which is shorter than its diff:
```python
import functools

import jax
import jax.numpy as jnp
from jax import lax
from jax.experimental import pallas as pl
from jax.experimental.pallas import tpu as pltpu
from jax.sharding import PartitionSpec as P

KEY = 64
VAL = 192
CONV_DILATION = 64
NT = 4
NX, NY, NZ, NC = 4, 4, 2, 2

eps_norm = 1e-05
root_half = 0.7071067811865476
inv_root_two_pi = 0.3989422804014327

MESH = pl.DeviceIdType.MESH
BF = jnp.bfloat16
F32 = jnp.float32
VMEM = pltpu.VMEM
VSPEC = pl.BlockSpec(memory_space=pltpu.VMEM)
HSPEC = pl.BlockSpec(memory_space=pltpu.HBM)


def normalize(values):
    average = jnp.mean(values, axis=-1, keepdims=True)
    centred = values - average
    inv_spread = lax.rsqrt(jnp.mean(centred * centred, axis=-1, keepdims=True) + eps_norm)
    return (centred * inv_spread, inv_spread)


def gelu_exact(values):
    return 0.5 * values * (1.0 + lax.erf(values * root_half))


def gelu_slope(values):
    return 0.5 * (1.0 + lax.erf(values * root_half)) + values * inv_root_two_pi * jnp.exp(
        -0.5 * values * values
    )


def seq_pos():
    s = lax.axis_index("seq")
    core = lax.rem(s, 2)
    z = lax.rem(lax.div(s, 2), 2)
    y = lax.rem(lax.div(s, 4), 4)
    x = lax.div(s, 16)
    return x, y, z, core


def seq_dev(x, y, z, core):
    return ((x * NY + y) * NZ + z) * NC + core


def nxt(i, k):
    return lax.rem(i + k, 4)


class Sender:
    def __init__(self, send_sems, recv_sems):
        self.ss, self.rs, self.n, self.flying = send_sems, recv_sems, 0, []

    def make(self, src, dst, dev):
        i = self.n
        self.n += 1
        return pltpu.make_async_remote_copy(
            src_ref=src,
            dst_ref=dst,
            send_sem=self.ss.at[i],
            recv_sem=self.rs.at[i],
            device_id=dev,
            device_id_type=MESH,
        )

    def go(self, src, dst, dev):
        c = self.make(src, dst, dev)
        c.start()
        self.flying.append(c)
        return c

    def drain(self):
        for c in self.flying:
            c.wait_send()
        self.flying = []


def greet(devs):
    barrier = pltpu.get_barrier_semaphore()
    for d in devs:
        pl.semaphore_signal(barrier, inc=1, device_id=d, device_id_type=MESH)
    pl.semaphore_wait(barrier, len(devs))


class Gather4:
    def __init__(self, sender, view, me, plus, minus, own=None):
        self.s, self.view, self.me, self.plus, self.minus = sender, view, me, plus, minus
        self.own = own or (lambda h: view(me, h))

    def begin(self):
        s, v, me, own = self.s, self.view, self.me, self.own
        self.c0 = s.go(own(0), v(me, 0), self.plus)
        self.c2 = s.go(own(1), v(me, 1), self.minus)
        self.c1 = s.go(own(1), v(me, 1), self.plus)
        self.c3 = s.go(own(0), v(me, 0), self.minus)

    def relay(self):
        s, v, me = self.s, self.view, self.me
        self.c0.wait_recv()
        self.c4 = s.go(v(nxt(me, 3), 0), v(nxt(me, 3), 0), self.plus)
        self.c2.wait_recv()
        self.c5 = s.go(v(nxt(me, 1), 1), v(nxt(me, 1), 1), self.minus)

    def wait_near(self):
        self.c1.wait_recv()
        self.c3.wait_recv()

    def wait_far(self):
        self.c4.wait_recv()
        self.c5.wait_recv()


class Reduce4:
    def __init__(self, sender, x, rbuf, me, plus, minus):
        self.s, self.x, self.r, self.me, self.plus, self.minus = sender, x, rbuf, me, plus, minus

    def begin(self):
        s, x, r, me = self.s, self.x, self.r, self.me
        self.a0 = s.go(x(nxt(me, 2), 0), r(0, 0), self.plus)
        self.a1 = s.go(x(nxt(me, 2), 1), r(1, 1), self.minus)
        self.b0 = s.go(x(nxt(me, 1), 1), r(2, 1), self.plus)
        self.b1 = s.go(x(nxt(me, 3), 0), r(3, 0), self.minus)

    def combine(self):
        s, x, r, me = self.s, self.x, self.r, self.me
        self.a0.wait_recv()
        t0 = r(6, 0)
        t0[...] = (x(nxt(me, 1), 0)[...].astype(F32) + r(0, 0)[...].astype(F32)).astype(BF)
        self.c0 = s.go(t0, r(4, 0), self.plus)
        self.a1.wait_recv()
        t1 = r(7, 1)
        t1[...] = (x(nxt(me, 3), 1)[...].astype(F32) + r(1, 1)[...].astype(F32)).astype(BF)
        self.c1 = s.go(t1, r(5, 1), self.minus)

    def finish(self):
        x, r, me = self.x, self.r, self.me
        self.b0.wait_recv()
        self.b1.wait_recv()
        self.c0.wait_recv()
        h0 = x(me, 0)[...].astype(F32) + r(3, 0)[...].astype(F32) + r(4, 0)[...].astype(F32)
        self.c1.wait_recv()
        h1 = x(me, 1)[...].astype(F32) + r(2, 1)[...].astype(F32) + r(5, 1)[...].astype(F32)
        return h0, h1


def tensor_ring():
    t = lax.axis_index("tensor")
    return t, {"tensor": nxt(t, 1)}, {"tensor": nxt(t, 3)}


def params(cid, mib):
    return pltpu.CompilerParams(
        collective_id=cid, has_side_effects=True, vmem_limit_bytes=mib * 1024 * 1024
    )


def seq_next(k):
    return {"seq": lax.rem(lax.axis_index("seq") + k, NX * NY * NZ * NC)}


def seq_prev():
    return seq_next(NX * NY * NZ * NC - 1)


def fetch(sem, i, src, dst):
    c = pltpu.make_async_copy(src, dst, sem.at[i])
    c.start()
    return c


def front_kernel(
    tok_hbm, cot_hbm, wq_hbm, wk_hbm, wv_hbm, ow_hbm, cw_hbm,
    att, full, cotx, terms_ref, owg,
    wq, wk, wv, cw, cots, qbuf, kvbuf, obuf, orecv, lbuf, lrecv, ss, rs, ls,
):
    x, y, z, core = seq_pos()
    t, plus, minus = tensor_ring()
    opposite = {"tensor": nxt(t, 2)}
    seqs, count, width = tok_hbm.shape
    rows = seqs * count
    half = count // 2
    edge = CONV_DILATION
    me = lax.axis_index("seq")
    last = NX * NY * NZ * NC - 1
    s = Sender(ss, rs)

    ltok = fetch(ls, 0, tok_hbm, full.at[t])
    lcot = fetch(ls, 1, cot_hbm, cotx.at[:, edge : edge + count])
    lcw = fetch(ls, 2, cw_hbm, cw)
    lws = [fetch(ls, 3, wq_hbm, wq), fetch(ls, 4, wk_hbm, wk), fetch(ls, 5, wv_hbm, wv)]
    partner = {"seq": seq_dev(x, y, z, 1 - core)}
    zpeer = {"seq": seq_dev(x, y, 1 - z, core)}
    xs = [{"seq": seq_dev(nxt(x, k), y, z, core)} for k in (1, 2, 3)]
    ys = [{"seq": seq_dev(x, nxt(y, k), z, core)} for k in (1, 2, 3)]
    axes = ((x, xs, y, ys), (y, ys, x, xs))
    greet([plus, minus, opposite, seq_next(1), seq_prev(), partner, zpeer] + xs + ys)

    def token_ring(i):
        return Gather4(
            s,
            lambda slot, h: full.at[slot, i, pl.ds(h * half, half)],
            t,
            plus,
            minus,
            own=lambda h: tok_hbm.at[i, pl.ds(h * half, half)],
        )

    def weight_gather():
        srows = ow_hbm.shape[0] // 8
        scols = ow_hbm.shape[1] // 4

        def pick(u, v):
            return jnp.where(core == 0, u, v)

        a, b = pick(x, y), pick(y, x)

        def dev(u, v):
            return {"seq": pick(u["seq"], v["seq"])}

        def rows_of(p):
            return pl.ds(pl.multiple_of((core * 4 + p) * srows, 16), srows)

        def cols_of(p):
            return pl.ds(pl.multiple_of(p * scols, 128), scols)

        zc = []
        for k, d in ((1, minus), (3, plus), (2, opposite)):
            piece = (rows_of(a), cols_of(b))
            zc.append(s.go(ow_hbm.at[piece], owg.at[(k - 1,) + piece], d))
        yield
        for c in zc:
            c.wait_recv()
        cut = (0, 32, srows)

        def view2(p, h):
            at = pl.multiple_of((core * 4 + a) * srows + cut[h], 16)
            return owg.at[:, pl.ds(at, cut[h + 1] - cut[h]), cols_of(p)]

        g2 = Gather4(s, view2, b, dev(ys[0], xs[0]), dev(ys[2], xs[2]))
        g2.begin()
        yield
        g2.relay()
        yield
        g2.wait_near()
        g2.wait_far()
        yield
        wide = ow_hbm.shape[1] // 2
        g1 = Gather4(
            s,
            lambda p, h: owg.at[:, rows_of(p), pl.ds(h * wide, wide)],
            a,
            dev(xs[0], ys[0]),
            dev(xs[2], ys[2]),
        )
        g1.begin()
        fw = []

        def forward(p):
            ref = owg.at[:, rows_of(p)]
            fw.append(s.go(ref, ref, partner))

        forward(a)
        yield
        g1.relay()
        yield
        g1.wait_near()
        forward(nxt(a, 1))
        forward(nxt(a, 3))
        yield
        g1.wait_far()
        forward(nxt(a, 2))
        yield
        for f in fw:
            f.wait_recv()

    def exchange(i):
        a, a_dev, b, b_dev = axes[i]
        own = kvbuf.at[i, a, z, core]
        cz = s.go(own, own, zpeer)

        def ring(zz):
            return Gather4(
                s,
                lambda slot, h: kvbuf.at[i, slot, zz, core, pl.ds(h * half, half)],
                a,
                a_dev[0],
                a_dev[2],
            )

        gk, go = ring(z), ring(1 - z)
        gq = Gather4(
            s, lambda slot, h: qbuf.at[i, slot, pl.ds(h * half, half)], b, b_dev[0], b_dev[2]
        )
        gk.begin()
        gq.begin()
        fw = []

        def forward(p, zz):
            ref = kvbuf.at[i, p, zz, core]
            fw.append(s.go(ref, ref, partner))

        forward(a, z)
        yield
        gk.relay()
        gq.relay()
        yield
        cz.wait_recv()
        go.begin()
        forward(a, 1 - z)
        yield
        gk.wait_near()
        forward(nxt(a, 1), z)
        forward(nxt(a, 3), z)
        yield
        gk.wait_far()
        forward(nxt(a, 2), z)
        go.relay()
        yield
        go.wait_near()
        forward(nxt(a, 1), 1 - z)
        forward(nxt(a, 3), 1 - z)
        yield
        go.wait_far()
        forward(nxt(a, 2), 1 - z)
        gq.wait_near()
        gq.wait_far()
        yield
        for f in fw:
            f.wait_recv()

    def project(i):
        a, _, b, _ = axes[i]
        values = jnp.concatenate([full[p, i] for p in range(NT)], axis=1).astype(F32)
        hidden = normalize(values)[0].astype(BF)
        qbuf[i, b] = jnp.dot(hidden, wq[...], preferred_element_type=F32).astype(BF)
        keys = wk.shape[1]
        kvbuf[i, a, z, core, :, 0:keys] = jnp.dot(
            hidden, wk[...], preferred_element_type=F32
        ).astype(BF)
        kvbuf[i, a, z, core, :, keys:] = jnp.dot(
            hidden, wv[...], preferred_element_type=F32
        ).astype(BF)

    def term(p):
        acc = jnp.zeros((rows, width), F32)
        for j in range(3):
            acc = acc + lax.dot_general(
                cots[j],
                cw[j, p * width : (p + 1) * width],
                (((1,), (1,)), ((), ())),
                preferred_element_type=F32,
            )
        terms_ref[p] = acc.astype(BF)

    keys = NX * NZ * NC * count
    lane2 = lax.broadcasted_iota(jnp.int32, (2 * count, 128), 1)
    lane = lax.broadcasted_iota(jnp.int32, (count, 128), 1)

    def attend(i, ks):
        b = axes[i][2]
        r0, r1 = nxt(b, ks[0]), nxt(b, ks[1])
        q = jnp.concatenate([qbuf[i, r0], qbuf[i, r1]], axis=0)
        q = (q.astype(F32) * KEY ** (-0.5)).astype(BF)
        k = kvbuf[i, :, :, :, :, 0:128].reshape(keys, 128)
        parts = []
        stats = jnp.zeros((2 * count, 128), F32)
        for h in range(2):
            qh = jnp.where((lane2 < KEY) if h == 0 else (lane2 >= KEY), q, jnp.zeros_like(q))
            sc = lax.dot_general(qh, k, (((1,), (1,)), ((), ())), preferred_element_type=F32)
            top = jnp.max(sc, axis=-1, keepdims=True)
            w = jnp.exp(sc - top)
            total = jnp.sum(w, axis=-1, keepdims=True)
            v = kvbuf[i, :, :, :, :, 128 + 128 * h : 384 + 128 * h].reshape(keys, 256)
            acc = jnp.dot(w.astype(BF), v, preferred_element_type=F32) / total
            parts.append(acc)
            stats = jnp.where(lane2 == h, top + jnp.log(total), stats)
        mid = jnp.where(lane2 < 64, parts[0][:, 128:], parts[1][:, :128])
        for n, r in enumerate((r0, r1)):
            at = slice(n * count, (n + 1) * count)
            obuf[i, r, :, 0:128] = parts[0][at, :128].astype(BF)
            obuf[i, r, :, 128:256] = mid[at].astype(BF)
            obuf[i, r, :, 256:384] = parts[1][at, 128:].astype(BF)
            lbuf[i, r] = stats[at].T[0:8]

    osent = [[], []]

    def send_out(i, k):
        b, b_dev = axes[i][2], axes[i][3]
        dev = b_dev[k - 1]
        osent[i].append(s.go(obuf.at[i, nxt(b, k)], orecv.at[i, b], dev))
        osent[i].append(s.go(lbuf.at[i, nxt(b, k)], lrecv.at[i, b], dev))

    def combine(i):
        b = axes[i][2]
        orecv[i, b] = obuf[i, b]
        lrecv[i, b] = lbuf[i, b]
        for c in osent[i]:
            c.wait_recv()
        logs = []
        for r in range(4):
            wide = jnp.concatenate([lrecv[i, r], jnp.zeros((120, 128), F32)], axis=0).T
            logs.append([wide[:, h : h + 1] for h in range(2)])
        wts = []
        for h in range(2):
            top = logs[0][h]
            for r in range(1, 4):
                top = jnp.maximum(top, logs[r][h])
            e = [jnp.exp(logs[r][h] - top) for r in range(4)]
            total = e[0] + e[1] + e[2] + e[3]
            wts.append([er / total for er in e])
        for g in range(3):
            acc = jnp.zeros((count, 128), F32)
            for r in range(4):
                if g == 0:
                    w = wts[0][r]
                elif g == 2:
                    w = wts[1][r]
                else:
                    w = jnp.where(lane < 64, wts[0][r], wts[1][r])
                acc = acc + orecv[i, r, :, 128 * g : 128 * g + 128].astype(F32) * w
            att[t, i, :, 128 * g : 128 * g + 128] = acc.astype(BF)
        ring = Gather4(
            s, lambda slot, h: att.at[slot, i, pl.ds(h * half, half)], t, plus, minus
        )
        ring.begin()
        return ring

    def step(gen):
        next(gen, None)

    tok0, tok1 = token_ring(0), token_ring(1)
    tok0.begin()
    up = s.go(cot_hbm.at[:, count - edge : count], cotx.at[:, 0:edge], seq_next(1))
    down = s.go(cot_hbm.at[:, 0:edge], cotx.at[:, edge + count : 2 * edge + count], seq_prev())
    lcot.wait()
    up.wait_recv()
    down.wait_recv()

    @pl.when(me == 0)
    def _():
        cotx[:, 0:edge] = jnp.zeros((2, edge, width), BF)

    @pl.when(me == last)
    def _():
        cotx[:, edge + count : 2 * edge + count] = jnp.zeros((2, edge, width), BF)

    for j in range(3):
        cots[j] = cotx[:, (2 - j) * edge : (2 - j) * edge + count].reshape(rows, width)
    lcw.wait()
    term(0)
    tok0.relay()
    weights = weight_gather()
    step(weights)
    tok1.begin()
    for p in range(1, NT):
        term(p)
    ltok.wait()
    for c in lws:
        c.wait()
    tok0.wait_near()
    tok0.wait_far()
    project(0)
    ex0 = exchange(0)
    step(ex0)
    tok1.relay()
    step(weights)
    step(ex0)
    step(ex0)
    step(weights)
    tok1.wait_near()
    tok1.wait_far()
    project(1)
    ex1 = exchange(1)
    step(ex1)
    step(weights)
    step(ex0)
    step(ex0)
    step(ex1)
    step(ex0)
    step(ex1)
    step(ex0)
    step(ex0)
    attend(0, (2, 1))
    send_out(0, 2)
    send_out(0, 1)
    step(ex1)
    step(ex1)
    step(weights)
    attend(0, (3, 0))
    send_out(0, 3)
    step(ex1)
    step(ex1)
    step(weights)
    step(ex1)
    attend(1, (2, 1))
    send_out(1, 2)
    send_out(1, 1)
    ring0 = combine(0)
    step(weights)
    attend(1, (3, 0))
    send_out(1, 3)
    ring0.relay()
    step(weights)
    ring1 = combine(1)
    step(weights)
    ring1.relay()
    ring0.wait_near()
    ring0.wait_far()
    ring1.wait_near()
    ring1.wait_far()
    for gen in (ex0, ex1, weights):
        for _ in gen:
            pass
    s.drain()


def in_hbm(v):
    return pltpu.with_memory_space_constraint(v, pltpu.HBM)


def front(tokens, cot, wq, wk, wv, ow, cw):
    seqs, count, width = tokens.shape
    keys, vals = wk.shape[1], wv.shape[1]
    n = 12 + 2 + 3 + 16 + 2 * 27 + 12 + 12
    return pl.pallas_call(
        front_kernel,
        name="front",
        out_shape=(
            jax.ShapeDtypeStruct((NT, seqs, count, vals), BF),
            jax.ShapeDtypeStruct((NT, seqs, count, width), BF),
            jax.ShapeDtypeStruct((seqs, count + 2 * CONV_DILATION, width), BF),
            jax.ShapeDtypeStruct((NT, seqs * count, width), BF),
            jax.ShapeDtypeStruct((NT - 1,) + ow.shape, BF),
        ),
        in_specs=[HSPEC] * 7,
        out_specs=(VSPEC,) * 5,
        scratch_shapes=[
            VMEM(wq.shape, BF),
            VMEM(wk.shape, BF),
            VMEM(wv.shape, BF),
            VMEM(cw.shape, BF),
            VMEM((3, seqs * count, width), BF),
            VMEM((seqs, 4, count, keys), BF),
            VMEM((seqs, 4, NZ, NC, count, keys + vals), BF),
            VMEM((seqs, 4, count, vals), BF),
            VMEM((seqs, 4, count, vals), BF),
            VMEM((seqs, 4, 8, count), F32),
            VMEM((seqs, 4, 8, count), F32),
            pltpu.SemaphoreType.DMA((n,)),
            pltpu.SemaphoreType.DMA((n,)),
            pltpu.SemaphoreType.DMA((6,)),
        ],
        compiler_params=params(1, 28),
    )(*[in_hbm(v) for v in (tokens, cot, wq, wk, wv, ow, cw)])


def tail_kernel(
    att, full, cotx, terms, ow, owg, cw,
    block_out, out_ref, residual,
    ug_ref, rt, blk, units, cots, taps, halo, st,
    send, recv, sums, r1, mid, r2, fin, zrecv, ss, rs,
):
    x, y, z, core = seq_pos()
    t, plus, minus = tensor_ring()
    me = lax.axis_index("seq")
    last = NX * NY * NZ * NC - 1
    rows, local = terms.shape[1:]
    half = rows // 2
    width = NT * local
    edge = CONV_DILATION
    total = 3 * width
    mine = total // 2
    tile = 256
    tiles = mine // tile
    per_tap = width // tile

    def pick(u, v):
        return jnp.where(core == 0, u, v)

    a, b = pick(x, y), pick(y, x)

    def along_a(k):
        return {"seq": pick(seq_dev(nxt(x, k), y, z, core), seq_dev(x, nxt(y, k), z, core))}

    def along_b(k):
        return {"seq": pick(seq_dev(x, nxt(y, k), z, core), seq_dev(nxt(x, k), y, z, core))}

    partner = {"seq": seq_dev(x, y, z, 1 - core)}
    zpeer = {"seq": seq_dev(x, y, 1 - z, core)}
    ap, am, bp, bm = along_a(1), along_a(3), along_b(1), along_b(3)
    opposite = {"tensor": nxt(t, 2)}
    after, before = seq_next(1), seq_prev()
    greet([plus, minus, opposite, partner, zpeer, ap, am, bp, bm, after, before])

    s = Sender(ss, rs)
    s.n = tiles

    red = Reduce4(
        s,
        lambda p, h: terms.at[p, pl.ds(h * half, half)],
        lambda i, h: rt.at[i],
        t,
        plus,
        minus,
    )
    red.begin()
    for j in range(3):
        cots[j] = cotx[:, (2 - j) * edge : (2 - j) * edge + half].reshape(rows, local)
    averages, invs = [], []
    for h in range(2):
        at = slice(h * half, (h + 1) * half)
        mixed = jnp.dot(att[t, h], ow[...], preferred_element_type=F32)
        for k in range(1, NT):
            mixed = mixed + jnp.dot(att[nxt(t, k), h], owg[k - 1], preferred_element_type=F32)
        for p in range(NT):
            blk[p, at] = (
                mixed[:, p * local : (p + 1) * local] + full[p, h].astype(F32)
            ).astype(BF)
        values = jnp.concatenate([blk[i, at] for i in range(NT)], axis=1).astype(F32)
        average = jnp.mean(values, axis=-1, keepdims=True)
        centred = values - average
        inv = lax.rsqrt(jnp.mean(centred * centred, axis=-1, keepdims=True) + eps_norm)
        units[at] = gelu_exact(centred * inv).astype(BF)
        averages.append(average)
        invs.append(inv)
    red.combine()

    def product(q):
        tap = lax.div(q, per_tap)
        col = pl.multiple_of(lax.rem(q, per_tap) * tile, tile)
        return lax.dot_general(
            units[:, pl.ds(col, tile)],
            cots[tap],
            (((0,), (0,)), ((), ())),
            preferred_element_type=F32,
        )

    def exchange(i):
        return pltpu.make_async_remote_copy(
            src_ref=send.at[i],
            dst_ref=recv.at[i],
            send_sem=ss.at[i],
            recv_sem=rs.at[i],
            device_id=partner,
            device_id_type=MESH,
        )

    @pl.loop(0, tiles)
    def _(i):
        send[i] = product((1 - core) * tiles + i).astype(BF)
        exchange(i).start()

    @pl.loop(0, tiles)
    def _(i):
        own = product(core * tiles + i)
        exchange(i).wait_recv()
        row = pl.multiple_of(i * tile, tile)
        sums[pl.ds(row, tile)] = (own + recv[i].astype(F32)).astype(BF)

    big = mine // 4
    small = big // 4
    bh = (0, big // 2)
    bn = (big // 2, big // 2)
    cut = (small // 2 + 15) // 16 * 16
    sh = (0, cut)
    sn = (cut, small - cut)

    def m16(v):
        return pl.multiple_of(v, 16)

    first = Reduce4(
        s,
        lambda p, h: sums.at[pl.ds(m16(p * big + bh[h]), bn[h])],
        lambda i, h: r1.at[i],
        a,
        ap,
        am,
    )
    first.begin()


    def tap(j):
        return jnp.dot(units[...], cw[j], preferred_element_type=F32).reshape(2, half, local)

    taps[0] = tap(0)
    up = s.go(taps.at[0, :, half - edge : half], halo.at[0], after)
    taps[2] = tap(2)
    down = s.go(taps.at[2, :, 0:edge], halo.at[1], before)
    first.combine()
    taps[1] = tap(1)
    h0, h1 = first.finish()
    mid[0 : big // 2] = h0.astype(BF)
    mid[big // 2 : big] = h1.astype(BF)
    second = Reduce4(
        s,
        lambda p, h: mid.at[pl.ds(m16(p * small + sh[h]), sn[h])],
        lambda i, h: r2.at[i, pl.ds(0, sn[h])],
        b,
        bp,
        bm,
    )
    second.begin()
    parts = red.finish()
    for h in range(2):
        ug_ref[h * half : (h + 1) * half] = parts[h]
    lane = lax.broadcasted_iota(jnp.int32, (half, 128), 1)
    for h in range(2):
        at = pl.ds(h * half, half)
        n = (blk[t, at].astype(F32) - averages[h]) * invs[h]
        slope = ug_ref[h * half : (h + 1) * half] * gelu_slope(n)
        one = jnp.sum(slope, axis=-1, keepdims=True)
        two = jnp.sum(slope * n, axis=-1, keepdims=True)
        stats = jnp.where(lane == 0, one, jnp.where(lane == 1, two, 0.0))
        st[t, h] = stats.T[0:8]
    stat_copies = [s.go(st.at[t], st.at[t], d) for d in (plus, minus, opposite)]
    second.combine()
    h0, h1 = second.finish()
    fin[0:cut] = h0.astype(BF)
    fin[cut:small] = h1.astype(BF)
    cz = s.go(fin, zrecv, zpeer)
    up.wait_recv()
    down.wait_recv()

    for h in range(2):
        own = blk[t, pl.ds(h * half, half)].astype(F32) + taps[1, h]
        left = jnp.where(me == 0, 0.0, halo[0, h])
        right = jnp.where(me == last, 0.0, halo[1, h])
        block_out[h, 0:edge] = (own[:edge] + left + taps[2, h, edge:half]).astype(BF)
        block_out[h, edge:half] = (own[edge:] + taps[0, h, 0 : half - edge] + right).astype(BF)

    cz.wait_recv()
    scale = (rows * NX * NY * NZ * NC) ** (-0.5)
    at = core * mine + a * big + b * small
    out_ref[pl.ds(m16(at), small)] = (
        (fin[...].astype(F32) + zrecv[...].astype(F32)) * scale
    ).astype(BF)
    g2 = Gather4(
        s,
        lambda p, h: out_ref.at[pl.ds(m16(core * mine + a * big + p * small + sh[h]), sn[h])],
        b,
        bp,
        bm,
    )
    g2.begin()
    g2.relay()
    g2.wait_near()
    g2.wait_far()

    def block(p):
        return out_ref.at[pl.ds(m16(core * mine + p * big), big)]

    g1 = Gather4(
        s,
        lambda p, h: out_ref.at[pl.ds(m16(core * mine + p * big + bh[h]), bn[h])],
        a,
        ap,
        am,
    )
    g1.begin()
    fw = [s.go(block(a), block(a), partner)]
    for c in stat_copies:
        c.wait_recv()
    for h in range(2):
        at = pl.ds(h * half, half)
        n = (blk[t, at].astype(F32) - averages[h]) * invs[h]
        slope = ug_ref[h * half : (h + 1) * half] * gelu_slope(n)
        both = (st[0, h] + st[1, h] + st[2, h] + st[3, h]) * (1.0 / width)
        wide = jnp.concatenate([both, jnp.zeros((120, 128), F32)], axis=0).T
        grad = (slope - wide[:, 0:1] - n * wide[:, 1:2]) * invs[h]
        residual[h] = (cotx[h, edge : edge + half].astype(F32) + grad).astype(BF)
    g1.relay()
    g1.wait_near()
    for k in (1, 3):
        fw.append(s.go(block(nxt(a, k)), block(nxt(a, k)), partner))
    g1.wait_far()
    fw.append(s.go(block(nxt(a, 2)), block(nxt(a, 2)), partner))
    for f in fw:
        f.wait_recv()
    s.drain()

    @pl.loop(0, tiles)
    def _(i):
        exchange(i).wait_send()


def tail(attended, full, cotx, terms, out_weight, others, conv_weight):
    _, rows, local = terms.shape
    width = local * NT
    half = rows // 2
    edge = CONV_DILATION
    mine = 3 * width // 2
    big, small = mine // 4, mine // 16
    cut = (small // 2 + 15) // 16 * 16
    n = mine // 256 + 6 * 5 + 1 + 4 + 2 + 3
    return pl.pallas_call(
        tail_kernel,
        name="tail",
        out_shape=(
            jax.ShapeDtypeStruct((2, half, local), BF),
            jax.ShapeDtypeStruct((3 * width, local), BF),
            jax.ShapeDtypeStruct((2, half, local), BF),
        ),
        in_specs=[VSPEC] * 7,
        out_specs=(VSPEC,) * 3,
        scratch_shapes=[
            VMEM((rows, local), F32),
            VMEM((8, half, local), BF),
            VMEM((NT, rows, local), BF),
            VMEM((rows, width), BF),
            VMEM((3, rows, local), BF),
            VMEM((3, 2, half, local), F32),
            VMEM((2, 2, edge, local), F32),
            VMEM((NT, 2, 8, 128), F32),
            VMEM((mine // 256, 256, local), BF),
            VMEM((mine // 256, 256, local), BF),
            VMEM((mine, local), BF),
            VMEM((8, big // 2, local), BF),
            VMEM((big, local), BF),
            VMEM((8, cut, local), BF),
            VMEM((small, local), BF),
            VMEM((small, local), BF),
            pltpu.SemaphoreType.DMA((n,)),
            pltpu.SemaphoreType.DMA((n,)),
        ],
        compiler_params=params(3, 24),
    )(attended, full, cotx, terms, out_weight, others, conv_weight)


def body(tokens_in, query_weight, key_weight, value_weight, out_weight, conv_weight, cotangent):
    local = tokens_in.shape[2]
    attended, full, cotx, terms, others = front(
        tokens_in, cotangent, query_weight, key_weight, value_weight, out_weight, conv_weight
    )
    block_out, conv_grad, residual_grad = tail(
        attended, full, cotx, terms, out_weight, others, conv_weight
    )
    return (block_out, conv_grad.reshape(3, local * NT, local), residual_grad)


def solution(mesh):
    placed = (
        P(None, "seq", "tensor"),
        P(None, "tensor"),
        P(None, "tensor"),
        P(None, "tensor"),
        P("tensor", None),
        P(None, None, "tensor"),
        P(None, "seq", "tensor"),
    )
    return jax.shard_map(
        body,
        mesh=mesh,
        in_specs=placed,
        out_specs=(P(None, "seq", "tensor"), P(None, None, "tensor"), P(None, "seq", "tensor")),
        check_vma=False,
    )
```

time: 166 us -> 143 us (0.86)
  Pallas kernels: 155 us -> 139 us
  local copies, waits for them, and re-layouts: 10.3 us -> 3.16 us
    pallas_call x1, Pallas kernels: 84.1 us -> 61.2 us  [tail(): pl.pallas_call(tail_kernel, name='tail', out_shape=(jax.ShapeDtypeStruct(...]
    unnamed x21 -> x7, local copies, waits for them, and re-layouts: 10.3 us -> 3.16 us
    pallas_call x2 -> x1, Pallas kernels: 70.7 us -> 77.6 us  [front(): pl.pallas_call(front_kernel, name='front', out_shape=(jax.ShapeDtypeStruc...]
where the time goes in v3:
time: 143 us
  Pallas kernels  139 us (97%)
  local copies, waits for them, and re-layouts  3.16 us (2%)
    pallas_call x1, Pallas kernels, front(): pl.pallas_call(front_kernel, name='front', out_shape=(jax.ShapeDtypeStruc...  77.6 us
    pallas_call x1, Pallas kernels, tail(): pl.pallas_call(tail_kernel, name='tail', out_shape=(jax.ShapeDtypeStruct(...  61.2 us
    unnamed x7, local copies, waits for them, and re-layouts  3.16 us

profile of v3, /device:TPU:1, one launch (start us, length us, event | category | flops | bytes accessed | tf_op | source)
XLA Modules:
  0.0 142.6 jit_solution(12424481356531789994)
XLA Ops:
  0.6 0.0 copy-start
  0.6 0.0 copy-start.1
  0.7 77.6 %front.1 = (bf16[4,2,128,384]{3,2,1,0:T(8,128)(2,1)S(1)}, bf16[4,2,128,384]{3,2,1,0:T(8,128)(2,1)S(1)}, bf16[2,256,384]{2,1,0:T(8,128)(2,1)S(1)}, bf16[4,256,384...) custom-call(bf16[2,128,384]{2,1,0:T(8,128)(2,1)} %tok_hbm.1, bf16[2,128,384]{2,1,0:T(8,128)(2,1)} %cot_hbm.1, ...), custom_call_target="tpu_custom_call" | custom-call | tf_op jit(solution)/shard_map/front/pallas_call | solution.py:537
  78.2 0.0 copy-done
  78.3 0.0 copy-done.1
  78.3 61.2 %tail.1 = (bf16[2,128,384]{2,1,0:T(8,128)(2,1)S(1)}, bf16[4608,384]{1,0:T(8,128)(2,1)S(1)}, bf16[2,128,384]{2,1,0:T(8,128)(2,1)S(1)}) custom-call(bf16[4,2,128,384]{3,2,1,0:T(8,128)(2,1)S(1)} %get-tuple-element.11.att, bf16[4,2,128,384]{3,2,1,0:T(8,128)(2,1)S(1)} %get-tuple-element.12.full, bf16[2,256,384]{2,1,0:T(8,128)(2,1)S(1)} %get-tuple-element.13.cotx, ...), custom_call_target="tpu_custom_call" | custom-call | tf_op jit(solution)/shard_map/tail/pallas_call | solution.py:807
  139.4 0.7 copy.13
  140.1 1.8 %copy.14 = bf16[3,1536,384]{2,1,0:T(8,128)(2,1)} copy(bf16[3,1536,384]{2,1,0:T(8,128)(2,1)S(1)} %bitcast.1) | data formatting | bytes 7077888
  141.9 0.7 copy.15
Async XLA Ops:
  0.6 77.6 %copy-start = (bf16[3,1536,384]{2,1,0:T(8,128)(2,1)S(1)}, bf16[3,1536,384]{2,1,0:T(8,128)(2,1)}, u32[]{:S(2)}) copy-start(bf16[3,1536,384]{2,1,0:T(8,128)(2,1)} %cw.1) | copy-start | bytes 10616836
  0.6 77.6 %copy-start.1 = (bf16[384,1536]{1,0:T(8,128)(2,1)S(1)}, bf16[384,1536]{1,0:T(8,128)(2,1)}, u32[]{:S(2)}) copy-start(bf16[384,1536]{1,0:T(8,128)(2,1)} %ow.1) | copy-start | bytes 3538948

commit v4 on v3

--- a/solution.py
+++ b/solution.py
@@ -469,16 +469,18 @@
     ltok.wait()
     for c in lws:
         c.wait()
+    step(weights)
     tok0.wait_near()
     tok0.wait_far()
+    tok1.relay()
     project(0)
     ex0 = exchange(0)
     step(ex0)
-    tok1.relay()
+    step(weights)
+    step(weights)
     step(weights)
     step(ex0)
     step(ex0)
-    step(weights)
     tok1.wait_near()
     tok1.wait_far()
     project(1)
@@ -486,35 +488,33 @@
     step(ex1)
     step(weights)
     step(ex0)
-    step(ex0)
     step(ex1)
     step(ex0)
     step(ex1)
     step(ex0)
+    step(weights)
+    step(ex0)
+    step(ex1)
+    step(weights)
     step(ex0)
     attend(0, (2, 1))
     send_out(0, 2)
     send_out(0, 1)
-    step(ex1)
     step(ex1)
     step(weights)
     attend(0, (3, 0))
     send_out(0, 3)
     step(ex1)
     step(ex1)
-    step(weights)
     step(ex1)
     attend(1, (2, 1))
     send_out(1, 2)
     send_out(1, 1)
     ring0 = combine(0)
-    step(weights)
     attend(1, (3, 0))
     send_out(1, 3)
     ring0.relay()
-    step(weights)
     ring1 = combine(1)
-    step(weights)
     ring1.relay()
     ring0.wait_near()
     ring0.wait_far()
@@ -589,20 +589,24 @@
     def pick(u, v):
         return jnp.where(core == 0, u, v)
 
-    a, b = pick(x, y), pick(y, x)
-
-    def along_a(k):
-        return {"seq": pick(seq_dev(nxt(x, k), y, z, core), seq_dev(x, nxt(y, k), z, core))}
-
-    def along_b(k):
-        return {"seq": pick(seq_dev(x, nxt(y, k), z, core), seq_dev(nxt(x, k), y, z, core))}
-
+    def along_x(k):
+        return seq_dev(nxt(x, k), y, z, core)
+
+    def along_y(k):
+        return seq_dev(x, nxt(y, k), z, core)
+
+    xr = (x, {"seq": along_x(1)}, {"seq": along_x(3)})
+    yr = (y, {"seq": along_y(1)}, {"seq": along_y(3)})
+    xy = (
+        (pick(x, y), *({"seq": pick(along_x(k), along_y(k))} for k in (1, 3))),
+        (pick(y, x), *({"seq": pick(along_y(k), along_x(k))} for k in (1, 3))),
+    )
+    axis_order = ((xr, yr), (yr, xr), xy)
     partner = {"seq": seq_dev(x, y, z, 1 - core)}
     zpeer = {"seq": seq_dev(x, y, 1 - z, core)}
-    ap, am, bp, bm = along_a(1), along_a(3), along_b(1), along_b(3)
     opposite = {"tensor": nxt(t, 2)}
     after, before = seq_next(1), seq_prev()
-    greet([plus, minus, opposite, partner, zpeer, ap, am, bp, bm, after, before])
+    greet([plus, minus, opposite, partner, zpeer, *xr[1:], *yr[1:], after, before])
 
     s = Sender(ss, rs)
     s.n = tiles
@@ -667,7 +671,9 @@
         own = product(core * tiles + i)
         exchange(i).wait_recv()
         row = pl.multiple_of(i * tile, tile)
-        sums[pl.ds(row, tile)] = (own + recv[i].astype(F32)).astype(BF)
+        both = (own + recv[i].astype(F32)).astype(BF)
+        for w in range(3):
+            sums[w, pl.ds(row, tile)] = both[:, w * 128 : (w + 1) * 128]
 
     big = mine // 4
     small = big // 4
@@ -676,19 +682,98 @@
     cut = (small // 2 + 15) // 16 * 16
     sh = (0, cut)
     sn = (cut, small - cut)
+    scale = (rows * NX * NY * NZ * NC) ** (-0.5)
 
     def m16(v):
         return pl.multiple_of(v, 16)
 
-    first = Reduce4(
-        s,
-        lambda p, h: sums.at[pl.ds(m16(p * big + bh[h]), bn[h])],
-        lambda i, h: r1.at[i],
-        a,
-        ap,
-        am,
-    )
-    first.begin()
+    def wave(w):
+        (a, ap, am), (b, bp, bm) = axis_order[w]
+        base = core * mine
+        first = Reduce4(
+            s,
+            lambda p, h: sums.at[w, pl.ds(m16(p * big + bh[h]), bn[h])],
+            lambda i, h: r1.at[w, i],
+            a,
+            ap,
+            am,
+        )
+        first.begin()
+        yield
+        first.combine()
+        yield
+        h0, h1 = first.finish()
+        mid[w, 0 : big // 2] = h0.astype(BF)
+        mid[w, big // 2 : big] = h1.astype(BF)
+        second = Reduce4(
+            s,
+            lambda p, h: mid.at[w, pl.ds(m16(p * small + sh[h]), sn[h])],
+            lambda i, h: r2.at[w, i, pl.ds(0, sn[h])],
+            b,
+            bp,
+            bm,
+        )
+        second.begin()
+        yield
+        second.combine()
+        yield
+        h0, h1 = second.finish()
+        fin[w, 0:cut] = h0.astype(BF)
+        fin[w, cut:small] = h1.astype(BF)
+        cz = s.go(fin.at[w], zrecv.at[w], zpeer)
+        yield
+        cz.wait_recv()
+        out_ref[w, pl.ds(m16(base + a * big + b * small), small)] = (
+            (fin[w].astype(F32) + zrecv[w].astype(F32)) * scale
+        ).astype(BF)
+        g2 = Gather4(
+            s,
+            lambda p, h: out_ref.at[w, pl.ds(m16(base + a * big + p * small + sh[h]), sn[h])],
+            b,
+            bp,
+            bm,
+        )
+        g2.begin()
+        yield
+        g2.relay()
+        yield
+        g2.wait_near()
+        g2.wait_far()
+        g1 = Gather4(
+            s,
+            lambda p, h: out_ref.at[w, pl.ds(m16(base + p * big + bh[h]), bn[h])],
+            a,
+            ap,
+            am,
+        )
+        g1.begin()
+        fw = []
+
+        def forward(p):
+            ref = out_ref.at[w, pl.ds(m16(base + p * big), big)]
+            fw.append(s.go(ref, ref, partner))
+
+        forward(a)
+        yield
+        g1.relay()
+        yield
+        g1.wait_near()
+        forward(nxt(a, 1))
+        forward(nxt(a, 3))
+        yield
+        g1.wait_far()
+        forward(nxt(a, 2))
+        yield
+        for f in fw:
+            f.wait_recv()
+
+    runs = [wave(w) for w in range(3)]
+
+    def advance():
+        for run in runs:
+            next(run, None)
+
+    advance()
 
 
     def tap(j):
@@ -698,20 +783,9 @@
     up = s.go(taps.at[0, :, half - edge : half], halo.at[0], after)
     taps[2] = tap(2)
     down = s.go(taps.at[2, :, 0:edge], halo.at[1], before)
-    first.combine()
+    advance()
     taps[1] = tap(1)
-    h0, h1 = first.finish()
-    mid[0 : big // 2] = h0.astype(BF)
-    mid[big // 2 : big] = h1.astype(BF)
-    second = Reduce4(
-        s,
-        lambda p, h: mid.at[pl.ds(m16(p * small + sh[h]), sn[h])],
-        lambda i, h: r2.at[i, pl.ds(0, sn[h])],
-        b,
-        bp,
-        bm,
-    )
-    second.begin()
+    advance()
     parts = red.finish()
     for h in range(2):
         ug_ref[h * half : (h + 1) * half] = parts[h]
@@ -725,14 +799,9 @@
         stats = jnp.where(lane == 0, one, jnp.where(lane == 1, two, 0.0))
         st[t, h] = stats.T[0:8]
     stat_copies = [s.go(st.at[t], st.at[t], d) for d in (plus, minus, opposite)]
-    second.combine()
-    h0, h1 = second.finish()
-    fin[0:cut] = h0.astype(BF)
-    fin[cut:small] = h1.astype(BF)
-    cz = s.go(fin, zrecv, zpeer)
+    advance()
     up.wait_recv()
     down.wait_recv()
-
     for h in range(2):
         own = blk[t, pl.ds(h * half, half)].astype(F32) + taps[1, h]
         left = jnp.where(me == 0, 0.0, halo[0, h])
@@ -740,36 +809,8 @@
         block_out[h, 0:edge] = (own[:edge] + left + taps[2, h, edge:half]).astype(BF)
         block_out[h, edge:half] = (own[edge:] + taps[0, h, 0 : half - edge] + right).astype(BF)
 
-    cz.wait_recv()
-    scale = (rows * NX * NY * NZ * NC) ** (-0.5)
-    at = core * mine + a * big + b * small
-    out_ref[pl.ds(m16(at), small)] = (
-        (fin[...].astype(F32) + zrecv[...].astype(F32)) * scale
-    ).astype(BF)
-    g2 = Gather4(
-        s,
-        lambda p, h: out_ref.at[pl.ds(m16(core * mine + a * big + p * small + sh[h]), sn[h])],
-        b,
-        bp,
-        bm,
-    )
-    g2.begin()
-    g2.relay()
-    g2.wait_near()
-    g2.wait_far()
-
-    def block(p):
-        return out_ref.at[pl.ds(m16(core * mine + p * big), big)]
-
-    g1 = Gather4(
-        s,
-        lambda p, h: out_ref.at[pl.ds(m16(core * mine + p * big + bh[h]), bn[h])],
-        a,
-        ap,
-        am,
-    )
-    g1.begin()
-    fw = [s.go(block(a), block(a), partner)]
+    advance()
+    advance()
     for c in stat_copies:
         c.wait_recv()
     for h in range(2):
@@ -780,14 +821,8 @@
         wide = jnp.concatenate([both, jnp.zeros((120, 128), F32)], axis=0).T
         grad = (slope - wide[:, 0:1] - n * wide[:, 1:2]) * invs[h]
         residual[h] = (cotx[h, edge : edge + half].astype(F32) + grad).astype(BF)
-    g1.relay()
-    g1.wait_near()
-    for k in (1, 3):
-        fw.append(s.go(block(nxt(a, k)), block(nxt(a, k)), partner))
-    g1.wait_far()
-    fw.append(s.go(block(nxt(a, 2)), block(nxt(a, 2)), partner))
-    for f in fw:
-        f.wait_recv()
+    for _ in range(7):
+        advance()
     s.drain()
 
     @pl.loop(0, tiles)
@@ -803,13 +838,13 @@
     mine = 3 * width // 2
     big, small = mine // 4, mine // 16
     cut = (small // 2 + 15) // 16 * 16
-    n = mine // 256 + 6 * 5 + 1 + 4 + 2 + 3
+    n = mine // 256 + 6 + 3 * (6 * 4 + 1 + 4) + 2 + 3
     return pl.pallas_call(
         tail_kernel,
         name="tail",
         out_shape=(
             jax.ShapeDtypeStruct((2, half, local), BF),
-            jax.ShapeDtypeStruct((3 * width, local), BF),
+            jax.ShapeDtypeStruct((local // 128, 3 * width, 128), BF),
             jax.ShapeDtypeStruct((2, half, local), BF),
         ),
         in_specs=[VSPEC] * 7,
@@ -825,17 +860,36 @@
             VMEM((NT, 2, 8, 128), F32),
             VMEM((mine // 256, 256, local), BF),
             VMEM((mine // 256, 256, local), BF),
-            VMEM((mine, local), BF),
-            VMEM((8, big // 2, local), BF),
-            VMEM((big, local), BF),
-            VMEM((8, cut, local), BF),
-            VMEM((small, local), BF),
-            VMEM((small, local), BF),
+            VMEM((3, mine, 128), BF),
+            VMEM((3, 8, big // 2, 128), BF),
+            VMEM((3, big, 128), BF),
+            VMEM((3, 8, cut, 128), BF),
+            VMEM((3, small, 128), BF),
+            VMEM((3, small, 128), BF),
             pltpu.SemaphoreType.DMA((n,)),
             pltpu.SemaphoreType.DMA((n,)),
         ],
         compiler_params=params(3, 24),
     )(attended, full, cotx, terms, out_weight, others, conv_weight)
+
+
+def side_by_side_kernel(parts, out):
+    for w in range(parts.shape[0]):
+        out[:, w * 128 : (w + 1) * 128] = parts[w]
+
+
+def side_by_side(parts):
+    n, rows, cols = parts.shape
+    step = rows // 6
+    return pl.pallas_call(
+        side_by_side_kernel,
+        name="side_by_side",
+        grid=(6,),
+        out_shape=jax.ShapeDtypeStruct((rows, n * cols), BF),
+        in_specs=[pl.BlockSpec((n, step, cols), lambda i: (0, i, 0))],
+        out_specs=pl.BlockSpec((step, n * cols), lambda i: (i, 0)),
+        compiler_params=pltpu.CompilerParams(vmem_limit_bytes=8 * 1024 * 1024),
+    )(parts)
 
 
 def body(tokens_in, query_weight, key_weight, value_weight, out_weight, conv_weight, cotangent):
@@ -846,7 +900,8 @@
     block_out, conv_grad, residual_grad = tail(
         attended, full, cotx, terms, out_weight, others, conv_weight
     )
-    return (block_out, conv_grad.reshape(3, local * NT, local), residual_grad)
+    conv_grad = side_by_side(conv_grad).reshape(3, local * NT, local)
+    return (block_out, conv_grad, residual_grad)
 
 
 def solution(mesh):

time: 143 us -> 148 us (1.035)
  Pallas kernels: 139 us -> 146 us
  local copies, waits for them, and re-layouts: 3.16 us -> 1.36 us
    pallas_call x1, Pallas kernels: 77.6 us -> 85.3 us  [front(): pl.pallas_call(front_kernel, name='front', out_shape=(jax.ShapeDtypeStruc...]
    pallas_call x1, Pallas kernels: 61.2 us -> 57.5 us  [tail(): pl.pallas_call(tail_kernel, name='tail', out_shape=(jax.ShapeDtypeStruct(...]
    pallas_call x0 -> x1, Pallas kernels: none -> 3.13 us  [side_by_side(): pl.pallas_call(side_by_side_kernel, name='side_by_side', grid=(6,), out_s...]
    unnamed x7 -> x6, local copies, waits for them, and re-layouts: 3.16 us -> 1.36 us
where the time goes in v4:
time: 148 us
  Pallas kernels  146 us (99%)
    pallas_call x1, Pallas kernels, front(): pl.pallas_call(front_kernel, name='front', out_shape=(jax.ShapeDtypeStruc...  85.3 us
    pallas_call x1, Pallas kernels, tail(): pl.pallas_call(tail_kernel, name='tail', out_shape=(jax.ShapeDtypeStruct(...  57.5 us
    pallas_call x1, Pallas kernels, side_by_side(): pl.pallas_call(side_by_side_kernel, name='side_by_side', grid=(6,), out_s...  3.13 us

profile of v4, /device:TPU:1, one launch (start us, length us, event | category | flops | bytes accessed | tf_op | source)
XLA Modules:
  0.0 148.0 jit_solution(79469951694381398)
XLA Ops:
  0.6 0.0 copy-start
  0.6 0.0 copy-start.1
  0.7 85.3 %front.1 = (bf16[4,2,128,384]{3,2,1,0:T(8,128)(2,1)S(1)}, bf16[4,2,128,384]{3,2,1,0:T(8,128)(2,1)S(1)}, bf16[2,256,384]{2,1,0:T(8,128)(2,1)S(1)}, bf16[4,256,384...) custom-call(bf16[2,128,384]{2,1,0:T(8,128)(2,1)} %tok_hbm.1, bf16[2,128,384]{2,1,0:T(8,128)(2,1)} %cot_hbm.1, ...), custom_call_target="tpu_custom_call" | custom-call | tf_op jit(solution)/shard_map/front/pallas_call | solution.py:537
  86.0 0.0 copy-done
  86.0 0.0 copy-done.1
  86.0 57.5 %tail.1 = (bf16[2,128,384]{2,1,0:T(8,128)(2,1)S(1)}, bf16[3,4608,128]{2,1,0:T(8,128)(2,1)S(1)}, bf16[2,128,384]{2,1,0:T(8,128)(2,1)S(1)}) custom-call(bf16[4,2,128,384]{3,2,1,0:T(8,128)(2,1)S(1)} %get-tuple-element.11.att, bf16[4,2,128,384]{3,2,1,0:T(8,128)(2,1)S(1)} %get-tuple-element.12.full, bf16[2,256,384]{2,1,0:T(8,128)(2,1)S(1)} %get-tuple-element.13.cotx, ...), custom_call_target="tpu_custom_call" | custom-call | tf_op jit(solution)/shard_map/tail/pallas_call | solution.py:842
  143.5 3.1 %side_by_side.1 = bf16[4608,384]{1,0:T(8,128)(2,1)} custom-call(bf16[3,4608,128]{2,1,0:T(8,128)(2,1)S(1)} %get-tuple-element.17.parts), custom_call_target="tpu_custom_call" | custom-call | tf_op jit(solution)/shard_map/side_by_side/pallas_call | solution.py:884
  146.7 0.7 copy.12
  147.3 0.7 copy.13
Async XLA Ops:
  0.6 85.4 %copy-start = (bf16[3,1536,384]{2,1,0:T(8,128)(2,1)S(1)}, bf16[3,1536,384]{2,1,0:T(8,128)(2,1)}, u32[]{:S(2)}) copy-start(bf16[3,1536,384]{2,1,0:T(8,128)(2,1)} %cw.1) | copy-start | bytes 10616836
  0.6 85.4 %copy-start.1 = (bf16[384,1536]{1,0:T(8,128)(2,1)S(1)}, bf16[384,1536]{1,0:T(8,128)(2,1)}, u32[]{:S(2)}) copy-start(bf16[384,1536]{1,0:T(8,128)(2,1)} %ow.1) | copy-start | bytes 3538948
